TPU v7x, 256 devices: a whole 4x4x8 slice. The times are simulated.
256 devices in a mesh: feat: 8 (over z), dom: 32 (over x, y, core).
Axes of the slice: x: 4, y: 4, z: 8, core: 2. Of those that a mesh axis runs over, the one named last changes fastest.
Arguments:
- features: bfloat16 [128, 32768], P('feat', 'dom'), may hold values from -6 to 6
- self_weight: bfloat16 [128, 512], P('feat'), may hold values from -0.5 to 0.5
- neighbor_weight: bfloat16 [128, 512], P('feat'), may hold values from -0.5 to 0.5
- unit_bias: float32 [512], P('feat'), may hold values from -3 to 3
- send_blocks: int32 [32, 32, 4], P('dom'), may hold values from 0 to 7
- send_counts: int32 [32, 32], P('dom'), may hold values from 0 to 4, as said below
- tile_target: int32 [32, 256], P('dom'), may hold values from 0 to 7
- tile_source: int32 [32, 256], P('dom'), may hold values from 0 to 135, as said below
- tile_count: int32 [32], P('dom'), may hold values from 64 to 256, as said below
- tile_weights: bfloat16 [32, 256, 128, 128], P('dom'), may hold values from 0 to 1, as said below
- out_grad: bfloat16 [512, 32768], P('feat', 'dom'), may hold values from -0.119628906 to 0.119628906
Outputs:
- hidden: bfloat16 [512, 32768], P('feat', 'dom')
- self_gradient: float32 [128, 512], P('feat')
- neighbor_gradient: float32 [128, 512], P('feat')
- bias_gradient: float32 [512], P('feat')
Inputs may be any that keep to these rules, and one draw needn't show every extreme that they name: `send_counts`: the diagonal is 0; each partition d fills all 4 slots toward partitions d - 1 and d + 1 (counted round). `tile_count`: at least one partition has all 256 tiles live. `tile_source`: tile 0 of partition d reads slot 8 + ((d + 1) mod 32) * 4, tile 1 reads slot 8 + ((d - 1) mod 32) * 4. `tile_weights`: entries may be 0.
All inputs are finite; a program needn't handle non-finite values.
Results may differ from a plain program's by a relative error of at most 0.005.
Values may be sent and summed in bfloat16 or wider, within the bound.
A program may use at most 64 MiB of HBM per device.

v0:
```python
import jax
import jax.numpy as jnp
from jax import lax
from jax.sharding import PartitionSpec as P

BLK = 128
BMAX = 4


def activate(values):
    return jax.nn.gelu(values, approximate=True)


def body(
    features,
    self_weight,
    neighbor_weight,
    unit_bias,
    send_blocks,
    send_counts,
    tile_target,
    tile_source,
    tile_count,
    tile_weights,
    out_grad,
):
    row_count = features.shape[1]
    unit_width = out_grad.shape[0]
    own_blocks = row_count // BLK
    neighbor_term = jnp.einsum(
        "fh,fr->hr", neighbor_weight, features, preferred_element_type=jnp.float32
    )
    self_term = jnp.einsum("fh,fr->hr", self_weight, features, preferred_element_type=jnp.float32)
    stacked = lax.psum_scatter(
        jnp.concatenate([neighbor_term, self_term], axis=1), "feat", scatter_dimension=0, tiled=True
    )
    projected = stacked[:, :row_count].astype(jnp.bfloat16)
    self_part = stacked[:, row_count:]
    slot_index = jnp.arange(BMAX, dtype=jnp.int32)
    chosen = send_blocks[0].reshape(-1)
    live_slots = (slot_index[None, :] < send_counts[0][:, None]).reshape(-1)
    own_table = projected.reshape(unit_width, own_blocks, BLK)
    outgoing = jnp.take(own_table, chosen, axis=1) * live_slots.astype(jnp.bfloat16)[None, :, None]
    incoming = lax.all_to_all(
        outgoing.reshape(unit_width, -1), "dom", split_axis=1, concat_axis=1, tiled=True
    )
    slot_table = jnp.concatenate([projected, incoming], axis=1).reshape(unit_width, -1, BLK)
    slot_number = slot_table.shape[1]
    weights = tile_weights[0]
    tile_total = weights.shape[0]
    live_tiles = (jnp.arange(tile_total, dtype=jnp.int32) < tile_count[0]).astype(jnp.float32)
    sources = tile_source[0]
    targets = tile_target[0]
    picked = jnp.take(slot_table, sources, axis=1)
    products = (
        jnp.einsum("htc,trc->thr", picked, weights, preferred_element_type=jnp.float32)
        * live_tiles[:, None, None]
    )
    block_sums = jax.ops.segment_sum(products, targets, num_segments=own_blocks)
    aggregate = jnp.transpose(block_sums, (1, 0, 2)).reshape(unit_width, row_count)
    unit_ones = jnp.ones((weights.shape[2],), jnp.bfloat16)
    row_sums = (
        jnp.einsum("trc,c->tr", weights, unit_ones, preferred_element_type=jnp.float32)
        * live_tiles[:, None]
    )
    degree = 1.0 + jax.ops.segment_sum(row_sums, targets, num_segments=own_blocks).reshape(
        row_count
    )
    summed_input = self_part + aggregate / degree[None, :] + unit_bias[:, None]
    hidden, pullback = jax.vjp(activate, summed_input)
    summed_grad = pullback(out_grad.astype(jnp.float32))[0]
    scaled = (summed_grad / degree[None, :]).astype(jnp.bfloat16)
    target_rows = jnp.take(scaled.reshape(unit_width, own_blocks, BLK), targets, axis=1)
    pushed = (
        jnp.einsum("htr,trc->thc", target_rows, weights, preferred_element_type=jnp.float32)
        * live_tiles[:, None, None]
    )
    slot_totals = jax.ops.segment_sum(pushed, sources, num_segments=slot_number)
    returned = lax.all_to_all(
        slot_totals[own_blocks:], "dom", split_axis=0, concat_axis=0, tiled=True
    )
    returned = returned * live_slots.astype(jnp.float32)[:, None, None]
    folded = (
        jax.ops.segment_sum(returned, chosen, num_segments=own_blocks) + slot_totals[:own_blocks]
    )
    neighbor_totals = (
        jnp.transpose(folded, (1, 0, 2)).reshape(unit_width, row_count).astype(jnp.bfloat16)
    )
    narrow_total = summed_grad.astype(jnp.bfloat16)
    bias_part = jnp.sum(summed_grad, axis=1)
    full_narrow, full_neighbor = (
        lax.all_gather(narrow_total, "feat", axis=0, tiled=True),
        lax.all_gather(neighbor_totals, "feat", axis=0, tiled=True),
    )
    self_term = jnp.einsum("fr,hr->fh", features, full_narrow, preferred_element_type=jnp.float32)
    neighbor_term = jnp.einsum(
        "fr,hr->fh", features, full_neighbor, preferred_element_type=jnp.float32
    )
    self_gradient, neighbor_gradient, bias_gradient = lax.psum(
        (self_term, neighbor_term, bias_part), "dom"
    )
    return (hidden.astype(jnp.bfloat16), self_gradient, neighbor_gradient, bias_gradient)


def solution(mesh):
    in_specs = (
        P("feat", "dom"),
        P("feat", None),
        P("feat", None),
        P("feat"),
        P("dom", None, None),
        P("dom", None),
        P("dom", None),
        P("dom", None),
        P("dom"),
        P("dom", None, None, None),
        P("feat", "dom"),
    )
    out_specs = (P("feat", "dom"), P("feat", None), P("feat", None), P("feat"))
    return jax.shard_map(body, mesh=mesh, in_specs=in_specs, out_specs=out_specs, check_vma=False)
```

profile of v0, /device:TPU:1, one launch (start us, length us, event | category | flops | bytes accessed | tf_op | source)
XLA Modules:
  0.0 458.2 jit_solution(16673961788908352427)
XLA Ops:
  7.9 1.2 fusion.48
  9.1 1.2 fusion.47
  10.3 2.4 pad_maximum_fusion
  14.1 58.0 %reduce-scatter.2.cloned.1.call-done = f32[64,2048]{1,0:T(8,128)} async-done(((f32[512,2048]{1,0:T(8,128)}), f32[64,2048]{1,0:T(8,128)}) %reduce-scatter.2.cloned.1.call-update) | async-done | bytes 524304 | tf_op jit(solution)/shard_map/reduce_scatter | solution.py:34
  74.0 2.7 copy.46
  76.7 3.1 gather.15
  80.0 2.5 copy.47
  82.5 7.5 %all-to-all-start = ((bf16[64,32,512]{2,0,1:T(8,128)(2,1)}), bf16[64,32,512]{2,0,1:T(8,128)(2,1)S(1)}, u32[]{:S(2)}, u32[]{:S(2)}) async-start(bf16[64,32,512]{2,0,1:T(8,128)(2,1)} %copy.47), calls=%async_computation.1 | async-start | bytes 4194304 | tf_op jit(solution)/shard_map/all_to_all | solution.py:44
  90.7 5.7 %fusion.2 = f32[1,256,128]{2,0,1:T(1,128)S(1)} fusion(bf16[1,256,128,128]{3,2,1,0:T(8,128)(2,1)} %param.20), kind=kOutput, calls=%fused_computation.9 | convolution fusion | flops 8388608 | bytes 8519680 | tf_op jit(solution)/shard_map/trc,c->tr/dot_general | solution.py:63
  96.4 2.2 scatter_custom_fusion.1
  98.7 19.6 %all-to-all-done = bf16[64,32,512]{2,0,1:T(8,128)(2,1)S(1)} async-done(((bf16[64,32,512]{2,0,1:T(8,128)(2,1)}), bf16[64,32,512]{2,0,1:T(8,128)(2,1)S(1)}, u32[]{:S(2)}, u32[]{:S(2)}) %all-to-all-start) | async-done | bytes 2097184 | tf_op jit(solution)/shard_map/all_to_all | solution.py:44
  119.1 3.1 gather_fusion.1
  122.2 13.6 %broadcast_multiply_fusion.1 = f32[256,64,128]{2,1,0:T(8,128)} fusion(f32[256]{0:T(256)S(1)} %get-tuple-element.14, bf16[1,256,128,128]{3,2,1,0:T(8,128)(2,1)} %param.20, bf16[256,64,128]{2,1,0:T(8,128)(2,1)} %gather_fusion.1, pred[256]{0:T(512)(128)(4,1)S(1)} %get-tuple-element.15), kind=kOutput, calls=%fused_computation.19 | convolution fusion | flops 541065216 | bytes 20972800 | tf_op jit(solution)/shard_map/htc,trc->thr/dot_general | solution.py:56
  135.9 26.2 %scatter_fusion = f32[8,64,128]{2,1,0:T(8,128)S(1)} fusion(f32[8,64,128]{2,1,0:T(8,128)S(1)} %broadcast.124, s32[256]{0:T(256)S(1)} %bitcast.115, f32[256,64,128]{2,1,0:T(8,128)} %broadcast_multiply_fusion.1), kind=kCustom, calls=%fused_computation.3 | custom fusion | flops 2097152 | bytes 25166848 | tf_op jit(solution)/shard_map/scatter-add | solution.py:59
  162.1 1.6 fusion.45
  164.4 3.1 gather_fusion.2
  167.4 10.4 %broadcast_multiply_fusion = f32[256,64,128]{2,1,0:T(8,128)} fusion(f32[256]{0:T(256)S(1)} %get-tuple-element.14, bf16[1,256,128,128]{3,2,1,0:T(8,128)(2,1)} %param.20, bf16[256,64,128]{2,1,0:T(8,128)(2,1)} %gather_fusion.2, pred[256]{0:T(512)(128)(4,1)S(1)} %compare_and_fusion), kind=kOutput, calls=%fused_computation.18 | convolution fusion | flops 541065216 | bytes 20972800 | tf_op jit(solution)/shard_map/htr,trc->thc/dot_general | solution.py:75
  177.8 2.6 broadcast_in_dim.58
  180.4 39.3 %scatter_fusion.1 = f32[136,64,128]{2,1,0:T(8,128)} fusion(f32[136,64,128]{2,1,0:T(8,128)} %broadcast_in_dim.58, s32[256]{0:T(256)S(1)} %bitcast.112, f32[256,64,128]{2,1,0:T(8,128)} %broadcast_multiply_fusion), kind=kCustom, calls=%fused_computation.5 | custom fusion | flops 2097152 | bytes 25166848 | tf_op jit(solution)/shard_map/scatter-add | solution.py:78
  219.7 4.7 %slice.26 = f32[128,64,128]{2,1,0:T(8,128)} slice(f32[136,64,128]{2,1,0:T(8,128)} %scatter_fusion.1), slice={[8:136], [0:64], [0:128]} | slice | bytes 8388608 | tf_op jit(solution)/shard_map/slice | solution.py:80
  224.5 5.4 %all-to-all-start.1 = ((f32[128,64,128]{2,1,0:T(8,128)}), f32[128,64,128]{2,1,0:T(8,128)}, u32[]{:S(2)}, u32[]{:S(2)}) async-start(f32[128,64,128]{2,1,0:T(8,128)} %slice.26), calls=%async_computation.2 | async-start | bytes 8388608 | tf_op jit(solution)/shard_map/all_to_all | solution.py:79
  230.9 1.0 slice.25
  231.8 50.3 %all-to-all-done.1 = f32[128,64,128]{2,1,0:T(8,128)} async-done(((f32[128,64,128]{2,1,0:T(8,128)}), f32[128,64,128]{2,1,0:T(8,128)}, u32[]{:S(2)}, u32[]{:S(2)}) %all-to-all-start.1) | async-done | bytes 4194336 | tf_op jit(solution)/shard_map/all_to_all | solution.py:79
  282.1 4.5 broadcast_multiply_fusion.2
  286.6 13.5 %scatter_fusion.2 = f32[8,64,128]{2,1,0:T(8,128)S(1)} fusion(f32[8,64,128]{2,1,0:T(8,128)S(1)} %slice.25, s32[128]{0:T(128)S(1)} %reshape.247, f32[128,64,128]{2,1,0:T(8,128)} %broadcast_multiply_fusion.2), kind=kCustom, calls=%fused_computation.6 | custom fusion | flops 1048576 | bytes 12583424 | tf_op jit(solution)/shard_map/scatter-add | solution.py:84
  301.0 2.2 convolution_bitcast_fusion.1
  303.2 29.7 %all-gather.5.cloned.1.call-done = bf16[512,1024]{1,0:T(8,128)(2,1)} async-done(((bf16[64,1024]{1,0:T(8,128)(2,1)}), bf16[512,1024]{1,0:T(8,128)(2,1)}) %all-gather.5.cloned.1.call-update) | async-done | bytes 1048592 | tf_op jit(solution)/shard_map/all_gather | solution.py:93
  332.9 2.2 convolution_bitcast_fusion
  335.2 112.6 %all-reduce.3.cloned.1.call-done = (f32[16,512]{1,0:T(8,128)}, f32[16,512]{1,0:T(8,128)}, f32[64]{0:T(128)}) async-done(((f32[16,512]{1,0:T(8,128)}, f32[16,512]{1,0:T(8,128)}, f32[64]{0:T(128)}), (f32[16,512]{1,0:T(8,128)}, f32[16,512]{1,0:T(8,128)}, f32[64]{0:T(128)})) %all-reduce.3.cloned.1.call-update) | async-done | bytes 65808 | tf_op jit(solution)/shard_map/psum | solution.py:99
  447.8 1.4 copy.85
  449.1 1.4 copy.86
  450.5 1.1 copy.87
  (54 shorter events, 7.5 us)
Async XLA Ops:
  7.2 0.8 copy-start
  7.2 64.9 %reduce-scatter.2.cloned.1.call-start = ((), (), s32[]{:S(2)}) async-start(), calls=%async_computation.3 | async-start | bytes 4718592 | tf_op jit(solution)/shard_map/reduce_scatter | solution.py:34
  12.7 0.7 copy-start.4
  12.7 1.1 copy-start.7
  80.0 10.6 %copy-start.3 = (s32[1,256]{1,0:T(1,128)S(1)}, s32[1,256]{1,0:T(1,128)}, u32[]{:S(2)}) copy-start(s32[1,256]{1,0:T(1,128)} %param.18) | copy-start | bytes 3076
  82.5 35.8 %all-to-all-start = ((bf16[64,32,512]{2,0,1:T(8,128)(2,1)}), bf16[64,32,512]{2,0,1:T(8,128)(2,1)S(1)}, u32[]{:S(2)}, u32[]{:S(2)}) async-start(bf16[64,32,512]{2,0,1:T(8,128)(2,1)} %copy.47), calls=%async_computation.1 | async-start | bytes 4194304 | tf_op jit(solution)/shard_map/all_to_all | solution.py:44
  90.7 5.7 %copy-start.5 = (s32[1,256]{1,0:T(1,128)S(1)}, s32[1,256]{1,0:T(1,128)}, u32[]{:S(2)}) copy-start(s32[1,256]{1,0:T(1,128)} %param.17) | copy-start | bytes 3076
  90.7 8.0 %copy-start.1 = (f32[64,2048]{1,0:T(8,128)S(1)}, f32[64,2048]{1,0:T(8,128)}, u32[]{:S(2)}) copy-start(f32[64,2048]{1,0:T(8,128)} %reduce-scatter.2.cloned.1.call-done) | copy-start | bytes 1572868
  135.8 26.3 %copy-start.2 = (bf16[64,1024]{1,0:T(8,128)(2,1)S(1)}, bf16[64,1024]{1,0:T(8,128)(2,1)}, u32[]{:S(2)}) copy-start(bf16[64,1024]{1,0:T(8,128)(2,1)} %param.21) | copy-start | bytes 393220
  135.8 26.3 %copy-start.6 = (f32[64]{0:T(128)S(1)}, f32[64]{0:T(128)}, u32[]{:S(2)}) copy-start(f32[64]{0:T(128)} %param.14) | copy-start | bytes 772
  224.5 57.7 %all-to-all-start.1 = ((f32[128,64,128]{2,1,0:T(8,128)}), f32[128,64,128]{2,1,0:T(8,128)}, u32[]{:S(2)}, u32[]{:S(2)}) async-start(f32[128,64,128]{2,1,0:T(8,128)} %slice.26), calls=%async_computation.2 | async-start | bytes 8388608 | tf_op jit(solution)/shard_map/all_to_all | solution.py:79
  229.9 71.1 %all-gather.3.cloned.1.call-start = ((), (), s32[]{:S(2)}) async-start(), calls=%async_computation.4 | async-start | bytes 1179648 | tf_op jit(solution)/shard_map/all_gather | solution.py:92
  230.6 102.3 %all-gather.5.cloned.1.call-start = ((), (), s32[]{:S(2)}) async-start(), calls=%async_computation.5 | async-start | bytes 1179648 | tf_op jit(solution)/shard_map/all_gather | solution.py:93
  300.9 146.9 %all-reduce.3.cloned.1.call-start = ((), (), s32[]{:S(2)}) async-start(), calls=%async_computation.6 | async-start | bytes 132096 | tf_op jit(solution)/shard_map/psum | solution.py:99
Sparse Core Ops, SparseCore 0:
  12.9 59.1 reduce-scatter.1
  232.5 33.6 all-gather.2
  301.0 31.8 all-gather.4
  337.0 110.7 all-reduce.2
where the time goes:
time: 460 us; the launch traced here: 458 us
  waiting for transfers between devices  271 us (59%)
  other arithmetic  92.1 us (20%)
  matrix products  36.5 us (8%)
  local copies, waits for them, and re-layouts  30.9 us (7%)
  between operations  14.7 us (3%)
  starting transfers between devices  13 us (3%)
    psum x1, waiting for transfers between devices, body(): lax.psum((self_term, neighbor_term, bias_part), 'dom')  113 us
    reduce_scatter x1, waiting for transfers between devices, body(): lax.psum_scatter(jnp.concatenate([neighbor_term, self_term], axis=1), 'fe...  58 us
    all_to_all x1, waiting for transfers between devices, body(): lax.all_to_all(slot_totals[own_blocks:], 'dom', split_axis=0, concat_axis...  50.3 us
    scatter-add x1, other arithmetic, body(): slot_totals = jax.ops.segment_sum(pushed, sources, num_segments=slot_number)  39.3 us
    all_gather x1, waiting for transfers between devices, body(): lax.all_gather(neighbor_totals, 'feat', axis=0, tiled=True)  29.7 us
    scatter-add x1, other arithmetic, body(): block_sums = jax.ops.segment_sum(products, targets, num_segments=own_blocks)  26.2 us
    all_to_all x1, waiting for transfers between devices, body(): lax.all_to_all(outgoing.reshape(unit_width, -1), 'dom', split_axis=1, con...  19.6 us
    dot_general x1, matrix products, body(): jnp.einsum('htc,trc->thr', picked, weights, preferred_element_type=jnp.fl...  13.6 us
  transfers between devices with their start and end apart: 6, of which 5 were waited for; matrix products, arithmetic and copies ran while one was open for 7% of the time, Pallas kernels for 0%

commit v1 on v0

v1 whole, which is shorter than its diff:
```python
import jax
import jax.numpy as jnp
from jax import lax
from jax.experimental import pallas as pl
from jax.experimental.pallas import tpu as pltpu
from jax.sharding import PartitionSpec as P

BLK = 128
BMAX = 4
NF = 8
ND = 32
RB = 8
NS = 136
TILES = 256
STEP = 8
FR = 16
HU = 64
PIECE = 4
MROWS = RB * FR + FR
BF = jnp.bfloat16
F32 = jnp.float32
MESH = pl.DeviceIdType.MESH
C0 = 0.7978845608028654
C1 = 0.044715


def dot_nt(a, b):
    return lax.dot_general(a, b, (((1,), (1,)), ((), ())), preferred_element_type=F32)


def dot_nn(a, b):
    return lax.dot_general(a, b, (((1,), (0,)), ((), ())), preferred_element_type=F32)


def split3(x):
    hi = x.astype(BF)
    rest = x - hi.astype(F32)
    mid = rest.astype(BF)
    low = (rest - mid.astype(F32)).astype(BF)
    return hi, mid, low


def kernel(
    feat_ref,
    sw_ref,
    nw_ref,
    bias_ref,
    blocks_ref,
    counts_ref,
    target_ref,
    source_ref,
    live_ref,
    tiles_ref,
    grad_ref,
    hidden_ref,
    selfg_ref,
    neighg_ref,
    biasg_ref,
    own,
    sendbuf,
    slots,
    wbuf,
    mask,
    ffull,
    wsend,
    wfull,
    wt,
    abuf,
    afull,
    ubuf,
    gbuf,
    hbuf,
    gsend,
    grecv,
    red,
    fin,
    tile_sem,
    local_sem,
    send_sem,
    recv_sem,
):
    f = lax.axis_index("feat")
    d = lax.axis_index("dom")

    barrier = pltpu.get_barrier_semaphore()

    def greet_dom(i, c):
        e = lax.rem(d + i, ND)
        pl.semaphore_signal(barrier, inc=1, device_id=(f, e), device_id_type=MESH)
        return c

    def greet_feat(i, c):
        g = lax.rem(f + i, NF)
        pl.semaphore_signal(barrier, inc=1, device_id=(g, d), device_id_type=MESH)
        return c

    lax.fori_loop(1, ND, greet_dom, 0)
    lax.fori_loop(1, NF, greet_feat, 0)

    def tile_copy(i):
        part = pl.ds(i * STEP, STEP)
        return pltpu.make_async_copy(tiles_ref.at[0, part], wbuf.at[part], tile_sem.at[i])

    def start_tiles(i, c):
        tile_copy(i).start()
        return c

    lax.fori_loop(0, TILES // STEP, start_tiles, 0)
    grad_copy = pltpu.make_async_copy(grad_ref, gbuf, local_sem.at[0])
    grad_copy.start()

    for b in range(RB):
        block = feat_ref[:, b * BLK : (b + 1) * BLK]
        own[b] = block
        slots[b] = block
        ffull[f, b] = block
    own[RB] = jnp.zeros((FR, BLK), BF)

    def fill(e, c):
        count = counts_ref[0, e]
        for k in range(BMAX):
            pick = jnp.where(k < count, blocks_ref[0, e, k], RB)
            sendbuf[e, k] = own[pick]
        return c

    lax.fori_loop(0, ND, fill, 0)
    slots[pl.ds(RB + BMAX * d, BMAX)] = sendbuf[d]

    for g in range(NF):
        wsend[g] = jnp.concatenate(
            [sw_ref[:, g * HU : (g + 1) * HU], nw_ref[:, g * HU : (g + 1) * HU]], axis=1
        )
    wfull[f] = wsend[f]

    pl.semaphore_wait(barrier, ND - 1 + NF - 1)

    def slot_copy(i):
        e = lax.rem(d + i, ND)
        return pltpu.make_async_remote_copy(
            src_ref=sendbuf.at[e],
            dst_ref=slots.at[pl.ds(RB + BMAX * d, BMAX)],
            send_sem=send_sem.at[0],
            recv_sem=recv_sem.at[0],
            device_id=(f, e),
            device_id_type=MESH,
        )

    def feat_copy(i):
        g = lax.rem(f + i, NF)
        return pltpu.make_async_remote_copy(
            src_ref=own.at[pl.ds(0, RB)],
            dst_ref=ffull.at[f],
            send_sem=send_sem.at[1],
            recv_sem=recv_sem.at[1],
            device_id=(g, d),
            device_id_type=MESH,
        )

    def weight_copy(i):
        g = lax.rem(f + i, NF)
        return pltpu.make_async_remote_copy(
            src_ref=wsend.at[g],
            dst_ref=wfull.at[f],
            send_sem=send_sem.at[2],
            recv_sem=recv_sem.at[2],
            device_id=(g, d),
            device_id_type=MESH,
        )

    def a_copy(i):
        g = lax.rem(f + i, NF)
        return pltpu.make_async_remote_copy(
            src_ref=abuf,
            dst_ref=afull.at[f],
            send_sem=send_sem.at[3],
            recv_sem=recv_sem.at[3],
            device_id=(g, d),
            device_id_type=MESH,
        )

    def part_copy(i):
        e = lax.rem(d + i, ND)
        return pltpu.make_async_remote_copy(
            src_ref=gsend.at[e],
            dst_ref=grecv.at[d],
            send_sem=send_sem.at[4],
            recv_sem=recv_sem.at[4],
            device_id=(f, e),
            device_id_type=MESH,
        )

    plane = d // PIECE
    place = lax.rem(d, PIECE)

    def fin_copy(i):
        e = lax.rem(d + i, ND)
        return pltpu.make_async_remote_copy(
            src_ref=red,
            dst_ref=fin.at[f, place],
            send_sem=send_sem.at[5],
            recv_sem=recv_sem.at[5],
            device_id=(plane, e),
            device_id_type=MESH,
        )

    def start(copy):
        def go(i, c):
            copy(i).start()
            return c

        return go

    def settle(ref, sem):
        pltpu.make_async_copy(ref, ref, sem).wait()

    lax.fori_loop(1, ND, start(slot_copy), 0)
    lax.fori_loop(1, NF, start(weight_copy), 0)
    lax.fori_loop(1, NF, start(feat_copy), 0)

    row = lax.broadcasted_iota(jnp.int32, (MROWS, BLK), 0)
    for j in range(RB):
        inside = ((row >= FR * j) & (row < FR * (j + 1))) | (row == RB * FR + j)
        mask[j] = jnp.where(inside, 1.0, 0.0).astype(BF)
    mask[RB] = jnp.zeros((MROWS, BLK), BF)

    wide = jnp.broadcast_to(bias_ref[...].reshape(1, HU), (BLK, HU))
    wide = jnp.concatenate([wide, jnp.zeros((BLK, BLK - HU), F32)], axis=1)
    bias_cols = jnp.transpose(wide)[:HU]

    settle(slots.at[pl.ds(RB, BMAX * (ND - 1))], recv_sem.at[0])

    live = live_ref[0]
    ones = jnp.ones((FR, BLK), BF)

    def step(i, total):
        tile_copy(i).wait()
        left, right = [], []
        for u in range(STEP):
            t = i * STEP + u
            chosen = slots[source_ref[0, t]]
            where = mask[jnp.where(t < live, target_ref[0, t], RB)]
            left.append(jnp.concatenate([chosen] * RB + [ones], axis=0) * where)
            right.append(wbuf[t])
        return total + dot_nt(jnp.concatenate(left, axis=1), jnp.concatenate(right, axis=1))

    total = lax.fori_loop(0, TILES // STEP, step, jnp.zeros((MROWS, BLK), F32))
    for b in range(RB):
        block = total[b * FR : (b + 1) * FR].astype(BF)
        abuf[b] = block
        afull[f, b] = block
    lax.fori_loop(1, NF, start(a_copy), 0)
    inverse = 1.0 / (1.0 + total[RB * FR : RB * FR + RB])

    settle(wfull.at[pl.ds(0, NF - 1)], recv_sem.at[2])
    settle(ffull.at[pl.ds(0, NF - 1)], recv_sem.at[1])
    wt[...] = jnp.transpose(wfull[...].reshape(NF * FR, BLK).astype(F32)).astype(BF)
    for b in range(RB):
        fb = ffull[:, b].reshape(NF * FR, BLK)
        ubuf[b] = dot_nn(wt[:HU], fb) + bias_cols
    grad_copy.wait()

    settle(afull.at[pl.ds(0, NF - 1)], recv_sem.at[3])

    gtotal = jnp.zeros((NF * FR, BLK), F32)
    btotal = jnp.zeros((HU, BLK), F32)
    nothing = jnp.zeros((HU, BLK), BF)
    for b in range(RB):
        fb = ffull[:, b].reshape(NF * FR, BLK)
        ab = afull[:, b].reshape(NF * FR, BLK)
        inv = inverse[b : b + 1]
        v = ubuf[b] + dot_nn(wt[HU:], ab) * inv
        v2 = v * v
        t = jnp.tanh(C0 * v * (1.0 + C1 * v2))
        half = 0.5 * (1.0 + t)
        hbuf[:, b * BLK : (b + 1) * BLK] = (v * half).astype(BF)
        slope = half + 0.5 * v * (1.0 - t * t) * (C0 * (1.0 + 3.0 * C1 * v2))
        grad = gbuf[:, b * BLK : (b + 1) * BLK].astype(F32) * slope
        btotal = btotal + grad
        narrow = grad.astype(BF)
        scaled = (grad * inv).astype(BF)
        right = jnp.concatenate(
            [
                jnp.concatenate([narrow, nothing], axis=1),
                jnp.concatenate([nothing, scaled], axis=1),
            ],
            axis=0,
        )
        gtotal = gtotal + dot_nt(jnp.concatenate([fb, ab], axis=1), right)
    hidden_copy = pltpu.make_async_copy(hbuf, hidden_ref, local_sem.at[1])
    hidden_copy.start()

    ones8 = jnp.ones((8, BLK), BF)
    brow = jnp.zeros((8, BLK), F32)
    for part in split3(btotal):
        brow = brow + dot_nt(ones8, jnp.concatenate([part, nothing], axis=0))
    for p in range(ND):
        gsend[p, :PIECE] = gtotal[p * PIECE : (p + 1) * PIECE]
        gsend[p, PIECE:] = brow[:PIECE]
    grecv[d] = gsend[d]
    lax.fori_loop(1, ND, start(part_copy), 0)
    settle(grecv.at[pl.ds(0, ND - 1)], recv_sem.at[4])

    added = grecv[0]
    for e in range(1, ND):
        added = added + grecv[e]
    red[...] = added
    biasg_ref[...] = added[PIECE : PIECE + 1, :HU]

    lax.fori_loop(1, ND, start(fin_copy), 0)

    @pl.when(plane != f)
    def _():
        fin_copy(0).start()

    @pl.when(plane == f)
    def _():
        fin[f, place] = red[...]

    @pl.when(plane == f)
    def _():
        settle(grecv.at[pl.ds(0, ND - 1)], recv_sem.at[5])

    @pl.when(plane != f)
    def _():
        settle(grecv, recv_sem.at[5])

    low = lax.broadcasted_iota(jnp.int32, (8, BLK), 0) < PIECE
    near = lax.broadcasted_iota(jnp.int32, (16, BLK), 1) < HU
    rows = []
    for g in range(NF):
        halves = []
        for q in range(0, 4, 2):
            halves.append(jnp.where(low, fin[g, q], pltpu.roll(fin[g, q + 1], 4, 0)))
        rows.append(jnp.concatenate(halves, axis=0))
    for j in range(NF // 2):
        a, b = rows[2 * j], rows[2 * j + 1]
        selfg_ref[:, j * BLK : (j + 1) * BLK] = jnp.where(near, a, pltpu.roll(b, HU, 1))
        neighg_ref[:, j * BLK : (j + 1) * BLK] = jnp.where(near, pltpu.roll(a, HU, 1), b)

    settle(sendbuf.at[pl.ds(0, ND - 1)], send_sem.at[0])
    settle(ffull.at[pl.ds(0, NF - 1)], send_sem.at[1])
    settle(wsend.at[pl.ds(0, NF - 1)], send_sem.at[2])
    settle(afull.at[pl.ds(0, NF - 1)], send_sem.at[3])
    settle(gsend.at[pl.ds(0, ND - 1)], send_sem.at[4])

    @pl.when(plane == f)
    def _():
        settle(gsend.at[pl.ds(0, ND - 1)], send_sem.at[5])

    @pl.when(plane != f)
    def _():
        settle(gsend, send_sem.at[5])

    hidden_copy.wait()


def body(
    features,
    self_weight,
    neighbor_weight,
    unit_bias,
    send_blocks,
    send_counts,
    tile_target,
    tile_source,
    tile_count,
    tile_weights,
    out_grad,
):
    vmem = pl.BlockSpec(memory_space=pltpu.VMEM)
    smem = pl.BlockSpec(memory_space=pltpu.SMEM)
    hbm = pl.BlockSpec(memory_space=pltpu.HBM)
    hidden, selfg, neighg, biasg = pl.pallas_call(
        kernel,
        out_shape=(
            jax.ShapeDtypeStruct((HU, RB * BLK), BF),
            jax.ShapeDtypeStruct((FR, NF * HU), F32),
            jax.ShapeDtypeStruct((FR, NF * HU), F32),
            jax.ShapeDtypeStruct((1, HU), F32),
        ),
        in_specs=[vmem, vmem, vmem, vmem, smem, smem, smem, smem, smem, hbm, hbm],
        out_specs=(hbm, vmem, vmem, vmem),
        scratch_shapes=[
            pltpu.VMEM((RB + 1, FR, BLK), BF),
            pltpu.VMEM((ND, BMAX, FR, BLK), BF),
            pltpu.VMEM((NS, FR, BLK), BF),
            pltpu.VMEM((TILES, BLK, BLK), BF),
            pltpu.VMEM((RB + 1, MROWS, BLK), BF),
            pltpu.VMEM((NF, RB, FR, BLK), BF),
            pltpu.VMEM((NF, FR, BLK), BF),
            pltpu.VMEM((NF, FR, BLK), BF),
            pltpu.VMEM((BLK, NF * FR), BF),
            pltpu.VMEM((RB, FR, BLK), BF),
            pltpu.VMEM((NF, RB, FR, BLK), BF),
            pltpu.VMEM((RB, HU, BLK), F32),
            pltpu.VMEM((HU, RB * BLK), BF),
            pltpu.VMEM((HU, RB * BLK), BF),
            pltpu.VMEM((ND, 8, BLK), F32),
            pltpu.VMEM((ND, 8, BLK), F32),
            pltpu.VMEM((8, BLK), F32),
            pltpu.VMEM((NF, PIECE, 8, BLK), F32),
            pltpu.SemaphoreType.DMA((TILES // STEP,)),
            pltpu.SemaphoreType.DMA((2,)),
            pltpu.SemaphoreType.DMA((6,)),
            pltpu.SemaphoreType.DMA((6,)),
        ],
        compiler_params=pltpu.CompilerParams(
            collective_id=0, has_side_effects=True, vmem_limit_bytes=40 << 20
        ),
    )(
        features,
        self_weight,
        neighbor_weight,
        unit_bias,
        send_blocks,
        send_counts,
        tile_target,
        tile_source,
        tile_count,
        tile_weights,
        out_grad,
    )
    return hidden, selfg, neighg, biasg.reshape(HU)


def solution(mesh):
    in_specs = (
        P("feat", "dom"),
        P("feat", None),
        P("feat", None),
        P("feat"),
        P("dom", None, None),
        P("dom", None),
        P("dom", None),
        P("dom", None),
        P("dom"),
        P("dom", None, None, None),
        P("feat", "dom"),
    )
    out_specs = (P("feat", "dom"), P("feat", None), P("feat", None), P("feat"))
    return jax.shard_map(body, mesh=mesh, in_specs=in_specs, out_specs=out_specs, check_vma=False)
```

time: 460 us -> 71.9 us (0.16)
  waiting for transfers between devices: 271 us -> 0 us
  other arithmetic: 92.1 us -> 0 us
  Pallas kernels: 0 us -> 57.9 us
  matrix products: 36.5 us -> 0 us
  local copies, waits for them, and re-layouts: 30.9 us -> 12.3 us
  between operations: 14.7 us -> 1.3 us
  starting transfers between devices: 13 us -> 0 us
    psum x1 -> x0, waiting for transfers between devices: 113 us -> none  [body(): lax.psum((self_term, neighbor_term, bias_part), 'dom')]
    scatter-add x4 -> x0, other arithmetic: 81.2 us -> none  [the longest x1 39.3 us: body(): slot_totals = jax.ops.segment_sum(pushed, sources, num_segments=slot_number)]
    all_to_all x2 -> x0, waiting for transfers between devices: 69.9 us -> none  [the longest x1 50.3 us: body(): lax.all_to_all(slot_totals[own_blocks:], 'dom', split_axis=0, concat_axis...]
    reduce_scatter x1 -> x0, waiting for transfers between devices: 58 us -> none  [body(): lax.psum_scatter(jnp.concatenate([neighbor_term, self_term], axis=1), 'fe...]
    pallas_call x0 -> x1, Pallas kernels: none -> 57.9 us  [body(): pl.pallas_call(kernel, out_shape=(jax.ShapeDtypeStruct((HU, RB * BLK), BF...]
    dot_general x7 -> x0, matrix products: 36.5 us -> none  [the longest x1 13.6 us: body(): jnp.einsum('htc,trc->thr', picked, weights, preferred_element_type=jnp.fl...]
    all_gather x2 -> x0, waiting for transfers between devices: 29.7 us -> none  [the longest x1 29.7 us: body(): lax.all_gather(neighbor_totals, 'feat', axis=0, tiled=True)]
    gather x5 -> x0, local copies, waits for them, and re-layouts: 12.9 us -> none  [the longest x3 6.74 us: body(): jnp.take(own_table, chosen, axis=1)]
  transfers between devices with their start and end apart: 6 -> 0, of which waited for: 5 -> 0; matrix products, arithmetic and copies ran while one was open for 7% -> 0% of each run, Pallas kernels for 0% -> 0%
where the time goes in v1:
time: 71.9 us; the launch traced here: 71.5 us
  Pallas kernels  57.9 us (81%)
  local copies, waits for them, and re-layouts  12.3 us (17%)
  between operations  1.3 us (2%)
    pallas_call x1, Pallas kernels, body(): pl.pallas_call(kernel, out_shape=(jax.ShapeDtypeStruct((HU, RB * BLK), BF...  57.9 us
    unnamed x23, local copies, waits for them, and re-layouts  12.3 us

profile of v1, /device:TPU:1, one launch (start us, length us, event | category | flops | bytes accessed | tf_op | source)
XLA Modules:
  0.0 71.5 jit_solution(7390638996001316361)
XLA Ops:
  1.3 0.8 %copy.15.blocks_ref = s32[1,32,4]{2,1,0:T(8,128)S(1)} copy(s32[1,32,4]{1,2,0:T(4,128)} %param.15) | data formatting | bytes 1024 | tf_op args[4]
  2.0 0.0 copy-start
  2.0 3.4 %copy-done = bf16[1,256,128,128]{3,2,1,0:T(8,128)(2,1)S(1)} copy-done((bf16[1,256,128,128]{3,2,1,0:T(8,128)(2,1)S(1)}, bf16[1,256,128,128]{3,2,1,0:T(8,128)(2,1)}, u32[]{:S(2)}) %copy-start) | copy-done | bytes 8388632
  5.4 0.0 copy-start.1
  5.4 0.9 %copy-done.1 = bf16[64,1024]{1,0:T(8,128)(2,1)S(1)} copy-done((bf16[64,1024]{1,0:T(8,128)(2,1)S(1)}, bf16[64,1024]{1,0:T(8,128)(2,1)}, u32[]{:S(2)}) %copy-start.1) | copy-done | bytes 131096
  6.3 0.0 copy-start.2
  6.3 0.8 %copy-done.2 = bf16[16,1024]{1,0:T(8,128)(2,1)S(1)} copy-done((bf16[16,1024]{1,0:T(8,128)(2,1)S(1)}, bf16[16,1024]{1,0:T(8,128)(2,1)}, u32[]{:S(2)}) %copy-start.2) | copy-done | bytes 32792
  7.1 0.0 copy-start.3
  7.1 0.7 copy-done.3
  7.8 0.0 copy-start.4
  7.8 0.7 copy-done.4
  8.5 0.0 copy-start.5
  8.5 0.7 copy-done.5
  9.2 0.0 copy-start.6
  9.2 0.7 copy-done.6
  9.9 0.0 copy-start.7
  9.9 0.7 copy-done.7
  10.5 0.0 copy-start.8
  10.5 0.7 copy-done.8
  11.2 57.9 %shard_map.138 = (bf16[64,1024]{1,0:T(8,128)(2,1)S(1)}, f32[16,512]{1,0:T(8,128)S(1)}, f32[16,512]{1,0:T(8,128)S(1)}, f32[1,64]{1,0:T(1,128)S(1)}) custom-call(bf16[16,1024]{1,0:T(8,128)(2,1)S(1)} %copy-done.2, bf16[16,512]{1,0:T(8,128)(2,1)S(1)} %copy-done.3, bf16[16,512]{1,0:T(8,128)(2,1)S(1)} %copy-done.4, f32[64]{0:T(128)S(1)} %copy-done.7, ...), custom_call_target="tpu_custom_call" | custom-call | tf_op jit(solution)/shard_map/pallas_call | solution.py:373
  69.1 0.7 copy.21
  69.8 0.6 copy.22
  70.4 0.6 copy.23
  71.0 0.5 copy.24
Async XLA Ops:
  2.0 3.4 %copy-start = (bf16[1,256,128,128]{3,2,1,0:T(8,128)(2,1)S(1)}, bf16[1,256,128,128]{3,2,1,0:T(8,128)(2,1)}, u32[]{:S(2)}) copy-start(bf16[1,256,128,128]{3,2,1,0:T(8,128)(2,1)} %tiles_ref.1) | copy-start | bytes 25165828
  5.4 0.9 %copy-start.1 = (bf16[64,1024]{1,0:T(8,128)(2,1)S(1)}, bf16[64,1024]{1,0:T(8,128)(2,1)}, u32[]{:S(2)}) copy-start(bf16[64,1024]{1,0:T(8,128)(2,1)} %grad_ref.1) | copy-start | bytes 393220
  6.3 0.8 %copy-start.2 = (bf16[16,1024]{1,0:T(8,128)(2,1)S(1)}, bf16[16,1024]{1,0:T(8,128)(2,1)}, u32[]{:S(2)}) copy-start(bf16[16,1024]{1,0:T(8,128)(2,1)} %feat_ref.1) | copy-start | bytes 98308
  7.1 0.7 %copy-start.3 = (bf16[16,512]{1,0:T(8,128)(2,1)S(1)}, bf16[16,512]{1,0:T(8,128)(2,1)}, u32[]{:S(2)}) copy-start(bf16[16,512]{1,0:T(8,128)(2,1)} %sw_ref.1) | copy-start | bytes 49156
  7.8 0.7 %copy-start.4 = (bf16[16,512]{1,0:T(8,128)(2,1)S(1)}, bf16[16,512]{1,0:T(8,128)(2,1)}, u32[]{:S(2)}) copy-start(bf16[16,512]{1,0:T(8,128)(2,1)} %nw_ref.1) | copy-start | bytes 49156
  8.5 0.7 copy-start.5
  9.2 0.7 copy-start.6
  9.9 0.7 copy-start.7
  10.5 0.7 copy-start.8

commit v2 on v1

--- a/solution.py
+++ b/solution.py
@@ -12,11 +12,11 @@
 RB = 8
 NS = 136
 TILES = 256
-STEP = 8
+STEP = 64
 FR = 16
 HU = 64
 PIECE = 4
-MROWS = RB * FR + FR
+MROWS = RB * FR
 BF = jnp.bfloat16
 F32 = jnp.float32
 MESH = pl.DeviceIdType.MESH
@@ -41,6 +41,21 @@
 
 
 def kernel(
+    feat_hbm,
+    sw_hbm,
+    nw_hbm,
+    bias_hbm,
+    blocks_hbm,
+    counts_hbm,
+    target_hbm,
+    source_hbm,
+    live_hbm,
+    tiles_ref,
+    grad_ref,
+    hidden_ref,
+    selfg_ref,
+    neighg_ref,
+    biasg_ref,
     feat_ref,
     sw_ref,
     nw_ref,
@@ -50,17 +65,12 @@
     target_ref,
     source_ref,
     live_ref,
-    tiles_ref,
-    grad_ref,
-    hidden_ref,
-    selfg_ref,
-    neighg_ref,
-    biasg_ref,
     own,
     sendbuf,
     slots,
     wbuf,
     mask,
+    rowmask,
     ffull,
     wsend,
     wfull,
@@ -74,6 +84,9 @@
     grecv,
     red,
     fin,
+    selfv,
+    neighv,
+    biasv,
     tile_sem,
     local_sem,
     send_sem,
@@ -82,6 +95,24 @@
     f = lax.axis_index("feat")
     d = lax.axis_index("dom")
 
+    loads = [
+        pltpu.make_async_copy(source, held, local_sem.at[2 + i])
+        for i, (source, held) in enumerate(
+            [
+                (feat_hbm, feat_ref),
+                (counts_hbm, counts_ref),
+                (blocks_hbm, blocks_ref),
+                (sw_hbm, sw_ref),
+                (nw_hbm, nw_ref),
+                (bias_hbm, bias_ref),
+                (target_hbm, target_ref),
+                (source_hbm, source_ref),
+                (live_hbm, live_ref),
+            ]
+        )
+    ]
+    for load in loads:
+        load.start()
     barrier = pltpu.get_barrier_semaphore()
 
     def greet_dom(i, c):
@@ -109,6 +140,8 @@
     grad_copy = pltpu.make_async_copy(grad_ref, gbuf, local_sem.at[0])
     grad_copy.start()
 
+    for load in loads:
+        load.wait()
     for b in range(RB):
         block = feat_ref[:, b * BLK : (b + 1) * BLK]
         own[b] = block
@@ -119,7 +152,7 @@
     def fill(e, c):
         count = counts_ref[0, e]
         for k in range(BMAX):
-            pick = jnp.where(k < count, blocks_ref[0, e, k], RB)
+            pick = jnp.where(k < count, blocks_ref[0, k, e], RB)
             sendbuf[e, k] = own[pick]
         return c
 
@@ -189,8 +222,11 @@
             device_id_type=MESH,
         )
 
-    plane = d // PIECE
-    place = lax.rem(d, PIECE)
+    core = lax.rem(d, 2)
+    column = lax.rem(d // 2, 4)
+    place = d // 8
+    shift = core * (7 - column) + (1 - core) * lax.rem(column + 1, 4)
+    plane = lax.rem(f + shift, NF)
 
     def fin_copy(i):
         e = lax.rem(d + i, ND)
@@ -218,10 +254,25 @@
     lax.fori_loop(1, NF, start(feat_copy), 0)
 
     row = lax.broadcasted_iota(jnp.int32, (MROWS, BLK), 0)
+    top = lax.broadcasted_iota(jnp.int32, (FR, BLK), 0)
     for j in range(RB):
-        inside = ((row >= FR * j) & (row < FR * (j + 1))) | (row == RB * FR + j)
-        mask[j] = jnp.where(inside, 1.0, 0.0).astype(BF)
+        mask[j] = jnp.where((row >= FR * j) & (row < FR * (j + 1)), 1.0, 0.0).astype(BF)
+        rowmask[j] = jnp.where(top == j, 1.0, 0.0).astype(BF)
     mask[RB] = jnp.zeros((MROWS, BLK), BF)
+    rowmask[RB] = jnp.zeros((FR, BLK), BF)
+    live = live_ref[0, 0]
+
+    def goal(t):
+        return jnp.where(t < live, target_ref[0, t], RB)
+
+    def degree_step(i, total):
+        tile_copy(i).wait()
+        left = [rowmask[goal(i * STEP + u)] for u in range(STEP)]
+        right = [wbuf[i * STEP + u] for u in range(STEP)]
+        return total + dot_nt(jnp.concatenate(left, axis=1), jnp.concatenate(right, axis=1))
+
+    degrees = lax.fori_loop(0, TILES // STEP, degree_step, jnp.zeros((FR, BLK), F32))
+    inverse = 1.0 / (1.0 + degrees)
 
     wide = jnp.broadcast_to(bias_ref[...].reshape(1, HU), (BLK, HU))
     wide = jnp.concatenate([wide, jnp.zeros((BLK, BLK - HU), F32)], axis=1)
@@ -229,17 +280,12 @@
 
     settle(slots.at[pl.ds(RB, BMAX * (ND - 1))], recv_sem.at[0])
 
-    live = live_ref[0]
-    ones = jnp.ones((FR, BLK), BF)
-
     def step(i, total):
-        tile_copy(i).wait()
         left, right = [], []
         for u in range(STEP):
             t = i * STEP + u
             chosen = slots[source_ref[0, t]]
-            where = mask[jnp.where(t < live, target_ref[0, t], RB)]
-            left.append(jnp.concatenate([chosen] * RB + [ones], axis=0) * where)
+            left.append(jnp.concatenate([chosen] * RB, axis=0) * mask[goal(t)])
             right.append(wbuf[t])
         return total + dot_nt(jnp.concatenate(left, axis=1), jnp.concatenate(right, axis=1))
 
@@ -249,7 +295,6 @@
         abuf[b] = block
         afull[f, b] = block
     lax.fori_loop(1, NF, start(a_copy), 0)
-    inverse = 1.0 / (1.0 + total[RB * FR : RB * FR + RB])
 
     settle(wfull.at[pl.ds(0, NF - 1)], recv_sem.at[2])
     settle(ffull.at[pl.ds(0, NF - 1)], recv_sem.at[1])
@@ -293,9 +338,14 @@
     brow = jnp.zeros((8, BLK), F32)
     for part in split3(btotal):
         brow = brow + dot_nt(ones8, jnp.concatenate([part, nothing], axis=0))
-    for p in range(ND):
-        gsend[p, :PIECE] = gtotal[p * PIECE : (p + 1) * PIECE]
-        gsend[p, PIECE:] = brow[:PIECE]
+    for g in range(NF):
+        away = lax.rem(g - f + NF, NF)
+        odd = away // 4
+        near = odd * (7 - away) + (1 - odd) * lax.rem(away + 3, 4)
+        for q in range(PIECE):
+            p = (q * 4 + near) * 2 + odd
+            gsend[p, :PIECE] = gtotal[g * FR + q * PIECE : g * FR + (q + 1) * PIECE]
+            gsend[p, PIECE:] = brow[:PIECE]
     grecv[d] = gsend[d]
     lax.fori_loop(1, ND, start(part_copy), 0)
     settle(grecv.at[pl.ds(0, ND - 1)], recv_sem.at[4])
@@ -303,39 +353,41 @@
     added = grecv[0]
     for e in range(1, ND):
         added = added + grecv[e]
-    red[...] = added
-    biasg_ref[...] = added[PIECE : PIECE + 1, :HU]
+    red[...] = added[:PIECE]
+    biasv[...] = added[PIECE : PIECE + 1, :HU]
+    bias_copy = pltpu.make_async_copy(biasv, biasg_ref, local_sem.at[11])
+    bias_copy.start()
 
     lax.fori_loop(1, ND, start(fin_copy), 0)
 
-    @pl.when(plane != f)
+    @pl.when(shift != 0)
     def _():
         fin_copy(0).start()
 
-    @pl.when(plane == f)
+    @pl.when(shift == 0)
     def _():
         fin[f, place] = red[...]
 
-    @pl.when(plane == f)
+    flat = fin.reshape(ND, PIECE, BLK)
+
+    @pl.when(shift == 0)
     def _():
-        settle(grecv.at[pl.ds(0, ND - 1)], recv_sem.at[5])
-
-    @pl.when(plane != f)
+        settle(flat.at[pl.ds(0, ND - 1)], recv_sem.at[5])
+
+    @pl.when(shift != 0)
     def _():
-        settle(grecv, recv_sem.at[5])
-
-    low = lax.broadcasted_iota(jnp.int32, (8, BLK), 0) < PIECE
-    near = lax.broadcasted_iota(jnp.int32, (16, BLK), 1) < HU
-    rows = []
-    for g in range(NF):
-        halves = []
-        for q in range(0, 4, 2):
-            halves.append(jnp.where(low, fin[g, q], pltpu.roll(fin[g, q + 1], 4, 0)))
-        rows.append(jnp.concatenate(halves, axis=0))
-    for j in range(NF // 2):
-        a, b = rows[2 * j], rows[2 * j + 1]
-        selfg_ref[:, j * BLK : (j + 1) * BLK] = jnp.where(near, a, pltpu.roll(b, HU, 1))
-        neighg_ref[:, j * BLK : (j + 1) * BLK] = jnp.where(near, pltpu.roll(a, HU, 1), b)
+        settle(flat, recv_sem.at[5])
+
+    rows = [jnp.concatenate([fin[g, q] for q in range(PIECE)], axis=0) for g in range(NF)]
+    for j in range(0, NF, 2):
+        a, b = rows[j], rows[j + 1]
+        at = slice(j * HU, (j + 2) * HU)
+        selfv[:, at] = jnp.concatenate([a[:, :HU], b[:, :HU]], axis=1)
+        neighv[:, at] = jnp.concatenate([a[:, HU:], b[:, HU:]], axis=1)
+    self_copy = pltpu.make_async_copy(selfv, selfg_ref, local_sem.at[12])
+    self_copy.start()
+    neigh_copy = pltpu.make_async_copy(neighv, neighg_ref, local_sem.at[13])
+    neigh_copy.start()
 
     settle(sendbuf.at[pl.ds(0, ND - 1)], send_sem.at[0])
     settle(ffull.at[pl.ds(0, NF - 1)], send_sem.at[1])
@@ -343,15 +395,26 @@
     settle(afull.at[pl.ds(0, NF - 1)], send_sem.at[3])
     settle(gsend.at[pl.ds(0, ND - 1)], send_sem.at[4])
 
-    @pl.when(plane == f)
+
+    @pl.when(shift == 0)
     def _():
-        settle(gsend.at[pl.ds(0, ND - 1)], send_sem.at[5])
-
-    @pl.when(plane != f)
+        settle(flat.at[pl.ds(0, ND - 1)], send_sem.at[5])
+
+    @pl.when(shift != 0)
     def _():
-        settle(gsend, send_sem.at[5])
-
-    hidden_copy.wait()
+        settle(flat, send_sem.at[5])
+
+    for copy in (bias_copy, hidden_copy, self_copy, neigh_copy):
+        copy.wait()
+
+
+def hand_over(*refs):
+    sems = refs[-1]
+    copies = [pltpu.make_async_copy(refs[i], refs[4 + i], sems.at[i]) for i in range(4)]
+    for copy in copies:
+        copy.start()
+    for copy in copies:
+        copy.wait()
 
 
 def body(
@@ -367,25 +430,34 @@
     tile_weights,
     out_grad,
 ):
-    vmem = pl.BlockSpec(memory_space=pltpu.VMEM)
-    smem = pl.BlockSpec(memory_space=pltpu.SMEM)
     hbm = pl.BlockSpec(memory_space=pltpu.HBM)
-    hidden, selfg, neighg, biasg = pl.pallas_call(
+    shapes = (
+        jax.ShapeDtypeStruct((HU, RB * BLK), BF),
+        jax.ShapeDtypeStruct((FR, NF * HU), F32),
+        jax.ShapeDtypeStruct((FR, NF * HU), F32),
+        jax.ShapeDtypeStruct((1, HU), F32),
+    )
+    made = pl.pallas_call(
         kernel,
-        out_shape=(
-            jax.ShapeDtypeStruct((HU, RB * BLK), BF),
-            jax.ShapeDtypeStruct((FR, NF * HU), F32),
-            jax.ShapeDtypeStruct((FR, NF * HU), F32),
-            jax.ShapeDtypeStruct((1, HU), F32),
-        ),
-        in_specs=[vmem, vmem, vmem, vmem, smem, smem, smem, smem, smem, hbm, hbm],
-        out_specs=(hbm, vmem, vmem, vmem),
+        out_shape=shapes,
+        in_specs=[hbm] * 11,
+        out_specs=(hbm,) * 4,
         scratch_shapes=[
+            pltpu.VMEM((FR, RB * BLK), BF),
+            pltpu.VMEM((FR, NF * HU), BF),
+            pltpu.VMEM((FR, NF * HU), BF),
+            pltpu.VMEM((HU,), F32),
+            pltpu.SMEM((1, BMAX, ND), jnp.int32),
+            pltpu.SMEM((1, ND), jnp.int32),
+            pltpu.SMEM((1, TILES), jnp.int32),
+            pltpu.SMEM((1, TILES), jnp.int32),
+            pltpu.SMEM((1, 1), jnp.int32),
             pltpu.VMEM((RB + 1, FR, BLK), BF),
             pltpu.VMEM((ND, BMAX, FR, BLK), BF),
             pltpu.VMEM((NS, FR, BLK), BF),
             pltpu.VMEM((TILES, BLK, BLK), BF),
             pltpu.VMEM((RB + 1, MROWS, BLK), BF),
+            pltpu.VMEM((RB + 1, FR, BLK), BF),
             pltpu.VMEM((NF, RB, FR, BLK), BF),
             pltpu.VMEM((NF, FR, BLK), BF),
             pltpu.VMEM((NF, FR, BLK), BF),
@@ -397,29 +469,39 @@
             pltpu.VMEM((HU, RB * BLK), BF),
             pltpu.VMEM((ND, 8, BLK), F32),
             pltpu.VMEM((ND, 8, BLK), F32),
-            pltpu.VMEM((8, BLK), F32),
-            pltpu.VMEM((NF, PIECE, 8, BLK), F32),
+            pltpu.VMEM((PIECE, BLK), F32),
+            pltpu.VMEM((NF, PIECE, PIECE, BLK), F32),
+            pltpu.VMEM((FR, NF * HU), F32),
+            pltpu.VMEM((FR, NF * HU), F32),
+            pltpu.VMEM((1, HU), F32),
             pltpu.SemaphoreType.DMA((TILES // STEP,)),
-            pltpu.SemaphoreType.DMA((2,)),
+            pltpu.SemaphoreType.DMA((14,)),
             pltpu.SemaphoreType.DMA((6,)),
             pltpu.SemaphoreType.DMA((6,)),
         ],
         compiler_params=pltpu.CompilerParams(
-            collective_id=0, has_side_effects=True, vmem_limit_bytes=40 << 20
+            collective_id=0, has_side_effects=True, vmem_limit_bytes=60 << 20
         ),
     )(
         features,
         self_weight,
         neighbor_weight,
         unit_bias,
-        send_blocks,
+        jnp.transpose(send_blocks, (0, 2, 1)),
         send_counts,
         tile_target,
         tile_source,
-        tile_count,
+        tile_count.reshape(1, 1),
         tile_weights,
         out_grad,
     )
+    hidden, selfg, neighg, biasg = pl.pallas_call(
+        hand_over,
+        out_shape=shapes,
+        in_specs=[hbm] * 4,
+        out_specs=(hbm,) * 4,
+        scratch_shapes=[pltpu.SemaphoreType.DMA((4,))],
+    )(*made)
     return hidden, selfg, neighg, biasg.reshape(HU)
 
 

time: 71.9 us -> 53.7 us (0.75)
  local copies, waits for them, and re-layouts: 12.3 us -> 0 us
  Pallas kernels: 57.9 us -> 52.3 us
    unnamed x23 -> x0, local copies, waits for them, and re-layouts: 12.3 us -> none
    pallas_call x1 -> x2, Pallas kernels: 57.9 us -> 52.3 us  [the longest x1 45.1 us: body(): pl.pallas_call(kernel, out_shape=shapes, in_specs=[hbm] * 11, out_specs=(...]
where the time goes in v2:
time: 53.7 us; the launch traced here: 53.5 us
  Pallas kernels  52.3 us (97%)
  between operations  1.29 us (2%)
    pallas_call x1, Pallas kernels, body(): pl.pallas_call(kernel, out_shape=shapes, in_specs=[hbm] * 11, out_specs=(...  45.1 us
    pallas_call x1, Pallas kernels, body(): pl.pallas_call(hand_over, out_shape=shapes, in_specs=[hbm] * 4, out_specs...  7.11 us

profile of v2, /device:TPU:1, one launch (start us, length us, event | category | flops | bytes accessed | tf_op | source)
XLA Modules:
  0.0 53.5 jit_solution(13321773564059517445)
XLA Ops:
  1.3 45.1 %shard_map.138 = (bf16[64,1024]{1,0:T(8,128)(2,1)}, f32[16,512]{1,0:T(8,128)}, f32[16,512]{1,0:T(8,128)}, f32[1,64]{1,0:T(1,128)}) custom-call(bf16[16,1024]{1,0:T(8,128)(2,1)} %feat_hbm.1, bf16[16,512]{1,0:T(8,128)(2,1)} %sw_hbm.1, bf16[16,512]{1,0:T(8,128)(2,1)} %nw_hbm.1, f32[64]{0:T(128)} %bias_hbm.1, s32[1,4,32]{2,1,0:T(4,128)} %bitcast.4, ...), custom_call_target="tpu_custom_call" | custom-call | tf_op jit(solution)/shard_map/pallas_call | solution.py:440
  46.4 7.1 %shard_map.139 = (bf16[64,1024]{1,0:T(8,128)(2,1)}, f32[16,512]{1,0:T(8,128)}, f32[16,512]{1,0:T(8,128)}, f32[1,64]{1,0:T(1,128)}) custom-call(bf16[64,1024]{1,0:T(8,128)(2,1)} %get-tuple-element.12.refs_0_, f32[16,512]{1,0:T(8,128)} %get-tuple-element.13.refs_1_, f32[16,512]{1,0:T(8,128)} %get-tuple-element.14.refs_2_, f32[1,64]{1,0:T(1,128)} %get-tuple-element.15.refs_3_), custom_call_target="tpu_custom_call" | custom-call | tf_op jit(solution)/shard_map/pallas_call | solution.py:498

commit v3 on v2

--- a/solution.py
+++ b/solution.py
@@ -409,12 +409,8 @@
 
 
 def hand_over(*refs):
-    sems = refs[-1]
-    copies = [pltpu.make_async_copy(refs[i], refs[4 + i], sems.at[i]) for i in range(4)]
-    for copy in copies:
-        copy.start()
-    for copy in copies:
-        copy.wait()
+    for made, out in zip(refs[:4], refs[4:]):
+        out[...] = made[...]
 
 
 def body(
@@ -431,6 +427,7 @@
     out_grad,
 ):
     hbm = pl.BlockSpec(memory_space=pltpu.HBM)
+    vmem = pl.BlockSpec(memory_space=pltpu.VMEM)
     shapes = (
         jax.ShapeDtypeStruct((HU, RB * BLK), BF),
         jax.ShapeDtypeStruct((FR, NF * HU), F32),
@@ -439,9 +436,9 @@
     )
     made = pl.pallas_call(
         kernel,
-        out_shape=shapes,
+        out_shape=tuple(pltpu.VMEM(one.shape, one.dtype) for one in shapes),
         in_specs=[hbm] * 11,
-        out_specs=(hbm,) * 4,
+        out_specs=(vmem,) * 4,
         scratch_shapes=[
             pltpu.VMEM((FR, RB * BLK), BF),
             pltpu.VMEM((FR, NF * HU), BF),
@@ -498,10 +495,9 @@
     hidden, selfg, neighg, biasg = pl.pallas_call(
         hand_over,
         out_shape=shapes,
-        in_specs=[hbm] * 4,
-        out_specs=(hbm,) * 4,
-        scratch_shapes=[pltpu.SemaphoreType.DMA((4,))],
-    )(*made)
+        in_specs=[vmem] * 4,
+        out_specs=(vmem,) * 4,
+    )(*[pltpu.with_memory_space_constraint(one, pltpu.VMEM) for one in made])
     return hidden, selfg, neighg, biasg.reshape(HU)
 
 

time: 53.7 us -> 47.1 us (0.88)
  Pallas kernels: 52.3 us -> 45.7 us
    pallas_call x2, Pallas kernels: 52.3 us -> 45.7 us  [the longest x1 45 us: body(): pl.pallas_call(kernel, out_shape=tuple((pltpu.VMEM(one.shape, one.dtype)...]
where the time goes in v3:
time: 47.1 us; the launch traced here: 46.9 us
  Pallas kernels  45.7 us (97%)
  between operations  1.29 us (3%)
    pallas_call x1, Pallas kernels, body(): pl.pallas_call(kernel, out_shape=tuple((pltpu.VMEM(one.shape, one.dtype)...  45 us

profile of v3, /device:TPU:1, one launch (start us, length us, event | category | flops | bytes accessed | tf_op | source)
XLA Modules:
  0.0 46.9 jit_solution(15275049981985770887)
XLA Ops:
  1.3 45.0 %shard_map.138 = (bf16[64,1024]{1,0:T(8,128)(2,1)S(1)}, f32[16,512]{1,0:T(8,128)S(1)}, f32[16,512]{1,0:T(8,128)S(1)}, f32[1,64]{1,0:T(1,128)S(1)}) custom-call(bf16[16,1024]{1,0:T(8,128)(2,1)} %feat_hbm.1, bf16[16,512]{1,0:T(8,128)(2,1)} %sw_hbm.1, bf16[16,512]{1,0:T(8,128)(2,1)} %nw_hbm.1, f32[64]{0:T(128)} %bias_hbm.1, s32[1,4,32]{2,1,0:T(4,128)} %bitcast.4, ...), custom_call_target="tpu_custom_call" | custom-call | tf_op jit(solution)/shard_map/pallas_call | solution.py:437
  46.3 0.7 %shard_map.139 = (bf16[64,1024]{1,0:T(8,128)(2,1)}, f32[16,512]{1,0:T(8,128)}, f32[16,512]{1,0:T(8,128)}, f32[1,64]{1,0:T(1,128)}) custom-call(bf16[64,1024]{1,0:T(8,128)(2,1)S(1)} %get-tuple-element.12.refs_0_, f32[16,512]{1,0:T(8,128)S(1)} %get-tuple-element.13.refs_1_, f32[16,512]{1,0:T(8,128)S(1)} %get-tuple-element.14.refs_2_, ...), custom_call_target="tpu_custom_call" | custom-call | tf_op jit(solution)/shard_map/pallas_call | solution.py:495

commit v4 on v3

--- a/solution.py
+++ b/solution.py
@@ -16,7 +16,20 @@
 FR = 16
 HU = 64
 PIECE = 4
-MROWS = RB * FR
+HALF = FR // 2
+MROWS = RB * HALF
+
+
+def around(n, i):
+    return min(i, n - i)
+
+
+PLANE = sorted(
+    ((x, y, c) for x in range(4) for y in range(4) for c in range(2)),
+    key=lambda p: (-around(4, p[0]) - around(4, p[1]), -p[2]),
+)
+OTHERS = [p for p in PLANE if any(p)]
+COLUMN = sorted(range(1, NF), key=lambda z: -around(NF, z))
 BF = jnp.bfloat16
 F32 = jnp.float32
 MESH = pl.DeviceIdType.MESH
@@ -68,6 +81,7 @@
     own,
     sendbuf,
     slots,
+    twice,
     wbuf,
     mask,
     rowmask,
@@ -142,22 +156,25 @@
 
     for load in loads:
         load.wait()
-    for b in range(RB):
-        block = feat_ref[:, b * BLK : (b + 1) * BLK]
-        own[b] = block
-        slots[b] = block
-        ffull[f, b] = block
-    own[RB] = jnp.zeros((FR, BLK), BF)
+    for h in range(2):
+        for b in range(RB):
+            block = feat_ref[h * HALF : (h + 1) * HALF, b * BLK : (b + 1) * BLK]
+            own[h, b] = block
+            slots[h, b] = block
+            ffull[h, f, b] = block
+        own[h, RB] = jnp.zeros((HALF, BLK), BF)
 
     def fill(e, c):
         count = counts_ref[0, e]
         for k in range(BMAX):
             pick = jnp.where(k < count, blocks_ref[0, k, e], RB)
-            sendbuf[e, k] = own[pick]
+            for h in range(2):
+                sendbuf[h, e, k] = own[h, pick]
         return c
 
     lax.fori_loop(0, ND, fill, 0)
-    slots[pl.ds(RB + BMAX * d, BMAX)] = sendbuf[d]
+    for h in range(2):
+        slots[h, pl.ds(RB + BMAX * d, BMAX)] = sendbuf[h, d]
 
     for g in range(NF):
         wsend[g] = jnp.concatenate(
@@ -167,96 +184,44 @@
 
     pl.semaphore_wait(barrier, ND - 1 + NF - 1)
 
-    def slot_copy(i):
-        e = lax.rem(d + i, ND)
+    x, y, k = d // 8, lax.rem(d // 2, 4), lax.rem(d, 2)
+
+    def plane_peer(p):
+        return (lax.rem(x + p[0], 4) * 4 + lax.rem(y + p[1], 4)) * 2 + lax.rem(k + p[2], 2)
+
+    def remote(source, held, stage, device):
         return pltpu.make_async_remote_copy(
-            src_ref=sendbuf.at[e],
-            dst_ref=slots.at[pl.ds(RB + BMAX * d, BMAX)],
-            send_sem=send_sem.at[0],
-            recv_sem=recv_sem.at[0],
-            device_id=(f, e),
+            src_ref=source,
+            dst_ref=held,
+            send_sem=send_sem.at[stage],
+            recv_sem=recv_sem.at[stage],
+            device_id=device,
             device_id_type=MESH,
         )
 
-    def feat_copy(i):
-        g = lax.rem(f + i, NF)
-        return pltpu.make_async_remote_copy(
-            src_ref=own.at[pl.ds(0, RB)],
-            dst_ref=ffull.at[f],
-            send_sem=send_sem.at[1],
-            recv_sem=recv_sem.at[1],
-            device_id=(g, d),
-            device_id_type=MESH,
-        )
-
-    def weight_copy(i):
-        g = lax.rem(f + i, NF)
-        return pltpu.make_async_remote_copy(
-            src_ref=wsend.at[g],
-            dst_ref=wfull.at[f],
-            send_sem=send_sem.at[2],
-            recv_sem=recv_sem.at[2],
-            device_id=(g, d),
-            device_id_type=MESH,
-        )
-
-    def a_copy(i):
-        g = lax.rem(f + i, NF)
-        return pltpu.make_async_remote_copy(
-            src_ref=abuf,
-            dst_ref=afull.at[f],
-            send_sem=send_sem.at[3],
-            recv_sem=recv_sem.at[3],
-            device_id=(g, d),
-            device_id_type=MESH,
-        )
-
-    def part_copy(i):
-        e = lax.rem(d + i, ND)
-        return pltpu.make_async_remote_copy(
-            src_ref=gsend.at[e],
-            dst_ref=grecv.at[d],
-            send_sem=send_sem.at[4],
-            recv_sem=recv_sem.at[4],
-            device_id=(f, e),
-            device_id_type=MESH,
-        )
-
-    core = lax.rem(d, 2)
-    column = lax.rem(d // 2, 4)
-    place = d // 8
-    shift = core * (7 - column) + (1 - core) * lax.rem(column + 1, 4)
+    place = x
+    shift = k * (7 - y) + (1 - k) * lax.rem(y + 1, 4)
     plane = lax.rem(f + shift, NF)
-
-    def fin_copy(i):
-        e = lax.rem(d + i, ND)
-        return pltpu.make_async_remote_copy(
-            src_ref=red,
-            dst_ref=fin.at[f, place],
-            send_sem=send_sem.at[5],
-            recv_sem=recv_sem.at[5],
-            device_id=(plane, e),
-            device_id_type=MESH,
-        )
-
-    def start(copy):
-        def go(i, c):
-            copy(i).start()
-            return c
-
-        return go
 
     def settle(ref, sem):
         pltpu.make_async_copy(ref, ref, sem).wait()
 
-    lax.fori_loop(1, ND, start(slot_copy), 0)
-    lax.fori_loop(1, NF, start(weight_copy), 0)
-    lax.fori_loop(1, NF, start(feat_copy), 0)
+    boundary = pl.ds(RB + BMAX * d, BMAX)
+    for h in range(2):
+        for p in OTHERS:
+            e = plane_peer(p)
+            remote(sendbuf.at[h, e], slots.at[h, boundary], h, (f, e)).start()
+    for i in COLUMN:
+        g = lax.rem(f + i, NF)
+        remote(wsend.at[g], wfull.at[f], 2, (g, d)).start()
+    for i in COLUMN:
+        g = lax.rem(f + i, NF)
+        remote(own.at[:, pl.ds(0, RB)], ffull.at[:, f], 3, (g, d)).start()
 
     row = lax.broadcasted_iota(jnp.int32, (MROWS, BLK), 0)
     top = lax.broadcasted_iota(jnp.int32, (FR, BLK), 0)
     for j in range(RB):
-        mask[j] = jnp.where((row >= FR * j) & (row < FR * (j + 1)), 1.0, 0.0).astype(BF)
+        mask[j] = jnp.where((row >= HALF * j) & (row < HALF * (j + 1)), 1.0, 0.0).astype(BF)
         rowmask[j] = jnp.where(top == j, 1.0, 0.0).astype(BF)
     mask[RB] = jnp.zeros((MROWS, BLK), BF)
     rowmask[RB] = jnp.zeros((FR, BLK), BF)
@@ -278,40 +243,60 @@
     wide = jnp.concatenate([wide, jnp.zeros((BLK, BLK - HU), F32)], axis=1)
     bias_cols = jnp.transpose(wide)[:HU]
 
-    settle(slots.at[pl.ds(RB, BMAX * (ND - 1))], recv_sem.at[0])
-
-    def step(i, total):
-        left, right = [], []
-        for u in range(STEP):
-            t = i * STEP + u
-            chosen = slots[source_ref[0, t]]
-            left.append(jnp.concatenate([chosen] * RB, axis=0) * mask[goal(t)])
-            right.append(wbuf[t])
-        return total + dot_nt(jnp.concatenate(left, axis=1), jnp.concatenate(right, axis=1))
-
-    total = lax.fori_loop(0, TILES // STEP, step, jnp.zeros((MROWS, BLK), F32))
+    def aggregate(h, c):
+        settle(slots.at[h, pl.ds(RB, BMAX * (ND - 1))], recv_sem.at[h])
+
+        def double(i, c):
+            for u in range(8):
+                block = slots[h, i * 8 + u]
+                twice[i * 8 + u, :HALF] = block
+                twice[i * 8 + u, HALF:] = block
+            return c
+
+        lax.fori_loop(0, NS // 8, double, 0)
+
+        def step(i, total):
+            left, right = [], []
+            for u in range(STEP):
+                t = i * STEP + u
+                chosen = twice[source_ref[0, t]]
+                left.append(jnp.concatenate([chosen] * (RB // 2), axis=0) * mask[goal(t)])
+                right.append(wbuf[t])
+            return total + dot_nt(jnp.concatenate(left, axis=1), jnp.concatenate(right, axis=1))
+
+        total = lax.fori_loop(0, TILES // STEP, step, jnp.zeros((MROWS, BLK), F32))
+        for b in range(RB):
+            block = total[b * HALF : (b + 1) * HALF].astype(BF)
+            abuf[h, b] = block
+            afull[h, f, b] = block
+        for i in COLUMN:
+            g = lax.rem(f + i, NF)
+            remote(abuf.at[h], afull.at[h, f], 4 + h, (g, d)).start()
+        return c
+
+    lax.fori_loop(0, 2, aggregate, 0)
+
+    settle(wfull.at[pl.ds(0, NF - 1)], recv_sem.at[2])
+    settle(ffull.at[:, pl.ds(0, NF - 1)], recv_sem.at[3])
+    wide = wfull[...].astype(F32)
+    wide = jnp.concatenate(
+        [wide[:, h * HALF : (h + 1) * HALF].reshape(NF * HALF, BLK) for h in range(2)], axis=0
+    )
+    wt[...] = jnp.transpose(wide).astype(BF)
     for b in range(RB):
-        block = total[b * FR : (b + 1) * FR].astype(BF)
-        abuf[b] = block
-        afull[f, b] = block
-    lax.fori_loop(1, NF, start(a_copy), 0)
-
-    settle(wfull.at[pl.ds(0, NF - 1)], recv_sem.at[2])
-    settle(ffull.at[pl.ds(0, NF - 1)], recv_sem.at[1])
-    wt[...] = jnp.transpose(wfull[...].reshape(NF * FR, BLK).astype(F32)).astype(BF)
-    for b in range(RB):
-        fb = ffull[:, b].reshape(NF * FR, BLK)
+        fb = ffull[:, :, b].reshape(NF * FR, BLK)
         ubuf[b] = dot_nn(wt[:HU], fb) + bias_cols
     grad_copy.wait()
 
-    settle(afull.at[pl.ds(0, NF - 1)], recv_sem.at[3])
+    for h in range(2):
+        settle(afull.at[h, pl.ds(0, NF - 1)], recv_sem.at[4 + h])
 
     gtotal = jnp.zeros((NF * FR, BLK), F32)
     btotal = jnp.zeros((HU, BLK), F32)
     nothing = jnp.zeros((HU, BLK), BF)
     for b in range(RB):
-        fb = ffull[:, b].reshape(NF * FR, BLK)
-        ab = afull[:, b].reshape(NF * FR, BLK)
+        fb = ffull[:, :, b].reshape(NF * FR, BLK)
+        ab = afull[:, :, b].reshape(NF * FR, BLK)
         inv = inverse[b : b + 1]
         v = ubuf[b] + dot_nn(wt[HU:], ab) * inv
         v2 = v * v
@@ -344,11 +329,14 @@
         near = odd * (7 - away) + (1 - odd) * lax.rem(away + 3, 4)
         for q in range(PIECE):
             p = (q * 4 + near) * 2 + odd
-            gsend[p, :PIECE] = gtotal[g * FR + q * PIECE : g * FR + (q + 1) * PIECE]
+            at = (q // 2) * NF * HALF + g * HALF + (q % 2) * PIECE
+            gsend[p, :PIECE] = gtotal[at : at + PIECE]
             gsend[p, PIECE:] = brow[:PIECE]
     grecv[d] = gsend[d]
-    lax.fori_loop(1, ND, start(part_copy), 0)
-    settle(grecv.at[pl.ds(0, ND - 1)], recv_sem.at[4])
+    for p in OTHERS:
+        e = plane_peer(p)
+        remote(gsend.at[e], grecv.at[d], 6, (f, e)).start()
+    settle(grecv.at[pl.ds(0, ND - 1)], recv_sem.at[6])
 
     added = grecv[0]
     for e in range(1, ND):
@@ -358,11 +346,12 @@
     bias_copy = pltpu.make_async_copy(biasv, biasg_ref, local_sem.at[11])
     bias_copy.start()
 
-    lax.fori_loop(1, ND, start(fin_copy), 0)
+    for p in OTHERS:
+        remote(red, fin.at[f, place], 7, (plane, plane_peer(p))).start()
 
     @pl.when(shift != 0)
     def _():
-        fin_copy(0).start()
+        remote(red, fin.at[f, place], 7, (plane, d)).start()
 
     @pl.when(shift == 0)
     def _():
@@ -372,11 +361,11 @@
 
     @pl.when(shift == 0)
     def _():
-        settle(flat.at[pl.ds(0, ND - 1)], recv_sem.at[5])
+        settle(flat.at[pl.ds(0, ND - 1)], recv_sem.at[7])
 
     @pl.when(shift != 0)
     def _():
-        settle(flat, recv_sem.at[5])
+        settle(flat, recv_sem.at[7])
 
     rows = [jnp.concatenate([fin[g, q] for q in range(PIECE)], axis=0) for g in range(NF)]
     for j in range(0, NF, 2):
@@ -389,20 +378,20 @@
     neigh_copy = pltpu.make_async_copy(neighv, neighg_ref, local_sem.at[13])
     neigh_copy.start()
 
-    settle(sendbuf.at[pl.ds(0, ND - 1)], send_sem.at[0])
-    settle(ffull.at[pl.ds(0, NF - 1)], send_sem.at[1])
+    for h in range(2):
+        settle(sendbuf.at[h, pl.ds(0, ND - 1)], send_sem.at[h])
+        settle(afull.at[h, pl.ds(0, NF - 1)], send_sem.at[4 + h])
     settle(wsend.at[pl.ds(0, NF - 1)], send_sem.at[2])
-    settle(afull.at[pl.ds(0, NF - 1)], send_sem.at[3])
-    settle(gsend.at[pl.ds(0, ND - 1)], send_sem.at[4])
-
+    settle(ffull.at[:, pl.ds(0, NF - 1)], send_sem.at[3])
+    settle(gsend.at[pl.ds(0, ND - 1)], send_sem.at[6])
 
     @pl.when(shift == 0)
     def _():
-        settle(flat.at[pl.ds(0, ND - 1)], send_sem.at[5])
+        settle(flat.at[pl.ds(0, ND - 1)], send_sem.at[7])
 
     @pl.when(shift != 0)
     def _():
-        settle(flat, send_sem.at[5])
+        settle(flat, send_sem.at[7])
 
     for copy in (bias_copy, hidden_copy, self_copy, neigh_copy):
         copy.wait()
@@ -449,18 +438,19 @@
             pltpu.SMEM((1, TILES), jnp.int32),
             pltpu.SMEM((1, TILES), jnp.int32),
             pltpu.SMEM((1, 1), jnp.int32),
-            pltpu.VMEM((RB + 1, FR, BLK), BF),
-            pltpu.VMEM((ND, BMAX, FR, BLK), BF),
+            pltpu.VMEM((2, RB + 1, HALF, BLK), BF),
+            pltpu.VMEM((2, ND, BMAX, HALF, BLK), BF),
+            pltpu.VMEM((2, NS, HALF, BLK), BF),
             pltpu.VMEM((NS, FR, BLK), BF),
             pltpu.VMEM((TILES, BLK, BLK), BF),
             pltpu.VMEM((RB + 1, MROWS, BLK), BF),
             pltpu.VMEM((RB + 1, FR, BLK), BF),
-            pltpu.VMEM((NF, RB, FR, BLK), BF),
+            pltpu.VMEM((2, NF, RB, HALF, BLK), BF),
             pltpu.VMEM((NF, FR, BLK), BF),
             pltpu.VMEM((NF, FR, BLK), BF),
             pltpu.VMEM((BLK, NF * FR), BF),
-            pltpu.VMEM((RB, FR, BLK), BF),
-            pltpu.VMEM((NF, RB, FR, BLK), BF),
+            pltpu.VMEM((2, RB, HALF, BLK), BF),
+            pltpu.VMEM((2, NF, RB, HALF, BLK), BF),
             pltpu.VMEM((RB, HU, BLK), F32),
             pltpu.VMEM((HU, RB * BLK), BF),
             pltpu.VMEM((HU, RB * BLK), BF),
@@ -473,8 +463,8 @@
             pltpu.VMEM((1, HU), F32),
             pltpu.SemaphoreType.DMA((TILES // STEP,)),
             pltpu.SemaphoreType.DMA((14,)),
-            pltpu.SemaphoreType.DMA((6,)),
-            pltpu.SemaphoreType.DMA((6,)),
+            pltpu.SemaphoreType.DMA((8,)),
+            pltpu.SemaphoreType.DMA((8,)),
         ],
         compiler_params=pltpu.CompilerParams(
             collective_id=0, has_side_effects=True, vmem_limit_bytes=60 << 20

time: 47.1 us -> 45 us (0.955)
  Pallas kernels: 45.7 us -> 43.5 us
    pallas_call x1, Pallas kernels: 45 us -> 42.8 us  [body(): pl.pallas_call(kernel, out_shape=tuple((pltpu.VMEM(one.shape, one.dtype)...]
where the time goes in v4:
time: 45 us; the launch traced here: 44.8 us
  Pallas kernels  43.5 us (97%)
  between operations  1.29 us (3%)
    pallas_call x1, Pallas kernels, body(): pl.pallas_call(kernel, out_shape=tuple((pltpu.VMEM(one.shape, one.dtype)...  42.8 us

profile of v4, /device:TPU:1, one launch (start us, length us, event | category | flops | bytes accessed | tf_op | source)
XLA Modules:
  0.0 44.8 jit_solution(13579412853975066506)
XLA Ops:
  1.3 42.8 %shard_map.138 = (bf16[64,1024]{1,0:T(8,128)(2,1)S(1)}, f32[16,512]{1,0:T(8,128)S(1)}, f32[16,512]{1,0:T(8,128)S(1)}, f32[1,64]{1,0:T(1,128)S(1)}) custom-call(bf16[16,1024]{1,0:T(8,128)(2,1)} %feat_hbm.1, bf16[16,512]{1,0:T(8,128)(2,1)} %sw_hbm.1, bf16[16,512]{1,0:T(8,128)(2,1)} %nw_hbm.1, f32[64]{0:T(128)} %bias_hbm.1, s32[1,4,32]{2,1,0:T(4,128)} %bitcast.4, ...), custom_call_target="tpu_custom_call" | custom-call | tf_op jit(solution)/shard_map/pallas_call | solution.py:426
  44.1 0.7 %shard_map.139 = (bf16[64,1024]{1,0:T(8,128)(2,1)}, f32[16,512]{1,0:T(8,128)}, f32[16,512]{1,0:T(8,128)}, f32[1,64]{1,0:T(1,128)}) custom-call(bf16[64,1024]{1,0:T(8,128)(2,1)S(1)} %get-tuple-element.12.refs_0_, f32[16,512]{1,0:T(8,128)S(1)} %get-tuple-element.13.refs_1_, f32[16,512]{1,0:T(8,128)S(1)} %get-tuple-element.14.refs_2_, ...), custom_call_target="tpu_custom_call" | custom-call | tf_op jit(solution)/shard_map/pallas_call | solution.py:485

commit v5 on v4

--- a/solution.py
+++ b/solution.py
@@ -1,3 +1,5 @@
+import functools
+
 import jax
 import jax.numpy as jnp
 from jax import lax
@@ -12,7 +14,8 @@
 RB = 8
 NS = 136
 TILES = 256
-STEP = 64
+STEP = 32
+LONG = 256
 FR = 16
 HU = 64
 PIECE = 4
@@ -28,8 +31,13 @@
     ((x, y, c) for x in range(4) for y in range(4) for c in range(2)),
     key=lambda p: (-around(4, p[0]) - around(4, p[1]), -p[2]),
 )
-OTHERS = [p for p in PLANE if any(p)]
 COLUMN = sorted(range(1, NF), key=lambda z: -around(NF, z))
+
+
+def step_of(t):
+    return lax.rem(10 - t + (t // 2) * (3 + 2 * lax.rem(t, 2)), 4)
+
+
 BF = jnp.bfloat16
 F32 = jnp.float32
 MESH = pl.DeviceIdType.MESH
@@ -84,7 +92,7 @@
     twice,
     wbuf,
     mask,
-    rowmask,
+    inverse,
     ffull,
     wsend,
     wfull,
@@ -92,15 +100,15 @@
     abuf,
     afull,
     ubuf,
+    vbuf,
+    narrow,
+    scaled,
+    gscratch,
     gbuf,
-    hbuf,
     gsend,
     grecv,
     red,
     fin,
-    selfv,
-    neighv,
-    biasv,
     tile_sem,
     local_sem,
     send_sem,
@@ -108,6 +116,25 @@
 ):
     f = lax.axis_index("feat")
     d = lax.axis_index("dom")
+
+    x, y, k = d // 8, lax.rem(d // 2, 4), lax.rem(d, 2)
+
+    def plane_peer(j):
+        p = PLANE[j]
+        return (lax.rem(x + p[0], 4) * 4 + lax.rem(y + p[1], 4)) * 2 + lax.rem(k + p[2], 2)
+
+    def column_peer(i):
+        return lax.rem(f + COLUMN[i], NF)
+
+    def each(count, send):
+        for i in range(count):
+            send(i)
+
+    barrier = pltpu.get_barrier_semaphore()
+    for j in range(ND - 1):
+        pl.semaphore_signal(barrier, inc=1, device_id=(f, plane_peer(j)), device_id_type=MESH)
+    for i in range(NF - 1):
+        pl.semaphore_signal(barrier, inc=1, device_id=(column_peer(i), d), device_id_type=MESH)
 
     loads = [
         pltpu.make_async_copy(source, held, local_sem.at[2 + i])
@@ -127,21 +154,6 @@
     ]
     for load in loads:
         load.start()
-    barrier = pltpu.get_barrier_semaphore()
-
-    def greet_dom(i, c):
-        e = lax.rem(d + i, ND)
-        pl.semaphore_signal(barrier, inc=1, device_id=(f, e), device_id_type=MESH)
-        return c
-
-    def greet_feat(i, c):
-        g = lax.rem(f + i, NF)
-        pl.semaphore_signal(barrier, inc=1, device_id=(g, d), device_id_type=MESH)
-        return c
-
-    lax.fori_loop(1, ND, greet_dom, 0)
-    lax.fori_loop(1, NF, greet_feat, 0)
-
     def tile_copy(i):
         part = pl.ds(i * STEP, STEP)
         return pltpu.make_async_copy(tiles_ref.at[0, part], wbuf.at[part], tile_sem.at[i])
@@ -184,11 +196,6 @@
 
     pl.semaphore_wait(barrier, ND - 1 + NF - 1)
 
-    x, y, k = d // 8, lax.rem(d // 2, 4), lax.rem(d, 2)
-
-    def plane_peer(p):
-        return (lax.rem(x + p[0], 4) * 4 + lax.rem(y + p[1], 4)) * 2 + lax.rem(k + p[2], 2)
-
     def remote(source, held, stage, device):
         return pltpu.make_async_remote_copy(
             src_ref=source,
@@ -208,73 +215,90 @@
 
     boundary = pl.ds(RB + BMAX * d, BMAX)
     for h in range(2):
-        for p in OTHERS:
-            e = plane_peer(p)
+
+        def send_slots(j, h=h):
+            e = plane_peer(j)
             remote(sendbuf.at[h, e], slots.at[h, boundary], h, (f, e)).start()
-    for i in COLUMN:
-        g = lax.rem(f + i, NF)
+
+        each(ND - 1, send_slots)
+
+    def send_inputs(i):
+        g = column_peer(i)
         remote(wsend.at[g], wfull.at[f], 2, (g, d)).start()
-    for i in COLUMN:
-        g = lax.rem(f + i, NF)
         remote(own.at[:, pl.ds(0, RB)], ffull.at[:, f], 3, (g, d)).start()
 
+    each(NF - 1, send_inputs)
+
     row = lax.broadcasted_iota(jnp.int32, (MROWS, BLK), 0)
-    top = lax.broadcasted_iota(jnp.int32, (FR, BLK), 0)
     for j in range(RB):
         mask[j] = jnp.where((row >= HALF * j) & (row < HALF * (j + 1)), 1.0, 0.0).astype(BF)
-        rowmask[j] = jnp.where(top == j, 1.0, 0.0).astype(BF)
     mask[RB] = jnp.zeros((MROWS, BLK), BF)
-    rowmask[RB] = jnp.zeros((FR, BLK), BF)
     live = live_ref[0, 0]
 
     def goal(t):
         return jnp.where(t < live, target_ref[0, t], RB)
 
-    def degree_step(i, total):
-        tile_copy(i).wait()
-        left = [rowmask[goal(i * STEP + u)] for u in range(STEP)]
-        right = [wbuf[i * STEP + u] for u in range(STEP)]
-        return total + dot_nt(jnp.concatenate(left, axis=1), jnp.concatenate(right, axis=1))
-
-    degrees = lax.fori_loop(0, TILES // STEP, degree_step, jnp.zeros((FR, BLK), F32))
-    inverse = 1.0 / (1.0 + degrees)
+    def fill_ones(i, c):
+        twice[i] = jnp.ones((FR, BLK), BF)
+        return c
+
+    lax.fori_loop(0, NS, fill_ones, 0)
 
     wide = jnp.broadcast_to(bias_ref[...].reshape(1, HU), (BLK, HU))
     wide = jnp.concatenate([wide, jnp.zeros((BLK, BLK - HU), F32)], axis=1)
     bias_cols = jnp.transpose(wide)[:HU]
 
-    def aggregate(h, c):
-        settle(slots.at[h, pl.ds(RB, BMAX * (ND - 1))], recv_sem.at[h])
-
-        def double(i, c):
-            for u in range(8):
-                block = slots[h, i * 8 + u]
-                twice[i * 8 + u, :HALF] = block
-                twice[i * 8 + u, HALF:] = block
-            return c
-
-        lax.fori_loop(0, NS // 8, double, 0)
+    def double(h, i, c):
+        for u in range(8):
+            block = slots[h, i * 8 + u]
+            twice[i * 8 + u, :HALF] = block
+            twice[i * 8 + u, HALF:] = block
+        return c
+
+    def aggregate(turn, c):
+        h = turn - 1
+
+        @pl.when(turn == 0)
+        def _():
+            for i in range(TILES // STEP):
+                tile_copy(i).wait()
+
+        @pl.when(turn > 0)
+        def _():
+            settle(slots.at[h, pl.ds(RB, BMAX * (ND - 1))], recv_sem.at[h])
+            lax.fori_loop(0, NS // 8, functools.partial(double, h), 0)
 
         def step(i, total):
             left, right = [], []
-            for u in range(STEP):
-                t = i * STEP + u
+            for u in range(LONG):
+                t = i * LONG + u
                 chosen = twice[source_ref[0, t]]
                 left.append(jnp.concatenate([chosen] * (RB // 2), axis=0) * mask[goal(t)])
                 right.append(wbuf[t])
             return total + dot_nt(jnp.concatenate(left, axis=1), jnp.concatenate(right, axis=1))
 
-        total = lax.fori_loop(0, TILES // STEP, step, jnp.zeros((MROWS, BLK), F32))
-        for b in range(RB):
-            block = total[b * HALF : (b + 1) * HALF].astype(BF)
-            abuf[h, b] = block
-            afull[h, f, b] = block
-        for i in COLUMN:
-            g = lax.rem(f + i, NF)
-            remote(abuf.at[h], afull.at[h, f], 4 + h, (g, d)).start()
-        return c
-
-    lax.fori_loop(0, 2, aggregate, 0)
+        total = lax.fori_loop(0, TILES // LONG, step, jnp.zeros((MROWS, BLK), F32))
+
+        @pl.when(turn == 0)
+        def _():
+            inverse[...] = 1.0 / (1.0 + total)
+
+        @pl.when(turn > 0)
+        def _():
+            for b in range(RB):
+                block = total[b * HALF : (b + 1) * HALF].astype(BF)
+                abuf[h, b] = block
+                afull[h, f, b] = block
+
+            def send_aggregate(i):
+                g = column_peer(i)
+                remote(abuf.at[h], afull.at[h, f], 4 + h, (g, d)).start()
+
+            each(NF - 1, send_aggregate)
+
+        return c
+
+    lax.fori_loop(0, 3, aggregate, 0)
 
     settle(wfull.at[pl.ds(0, NF - 1)], recv_sem.at[2])
     settle(ffull.at[:, pl.ds(0, NF - 1)], recv_sem.at[3])
@@ -283,75 +307,88 @@
         [wide[:, h * HALF : (h + 1) * HALF].reshape(NF * HALF, BLK) for h in range(2)], axis=0
     )
     wt[...] = jnp.transpose(wide).astype(BF)
+    fblocks = [ffull[:, :, b].reshape(NF * FR, BLK) for b in range(RB)]
+    uall = dot_nn(wt[:HU], jnp.concatenate(fblocks, axis=1))
     for b in range(RB):
-        fb = ffull[:, :, b].reshape(NF * FR, BLK)
-        ubuf[b] = dot_nn(wt[:HU], fb) + bias_cols
+        ubuf[b] = uall[:, b * BLK : (b + 1) * BLK] + bias_cols
     grad_copy.wait()
 
     for h in range(2):
         settle(afull.at[h, pl.ds(0, NF - 1)], recv_sem.at[4 + h])
 
-    gtotal = jnp.zeros((NF * FR, BLK), F32)
-    btotal = jnp.zeros((HU, BLK), F32)
+    ablocks = [afull[:, :, b].reshape(NF * FR, BLK) for b in range(RB)]
+    vall = dot_nn(wt[HU:], jnp.concatenate(ablocks, axis=1))
+    for b in range(RB):
+        vbuf[b] = vall[:, b * BLK : (b + 1) * BLK]
     nothing = jnp.zeros((HU, BLK), BF)
-    for b in range(RB):
-        fb = ffull[:, :, b].reshape(NF * FR, BLK)
-        ab = afull[:, :, b].reshape(NF * FR, BLK)
-        inv = inverse[b : b + 1]
-        v = ubuf[b] + dot_nn(wt[HU:], ab) * inv
+
+    def activate(b, btotal):
+        at = pl.ds(pl.multiple_of(b * BLK, BLK), BLK)
+        inv = inverse[pl.ds(pl.multiple_of(b * HALF, HALF), HALF)][:1]
+        v = ubuf[b] + vbuf[b] * inv
         v2 = v * v
         t = jnp.tanh(C0 * v * (1.0 + C1 * v2))
         half = 0.5 * (1.0 + t)
-        hbuf[:, b * BLK : (b + 1) * BLK] = (v * half).astype(BF)
+        hidden_ref[:, at] = (v * half).astype(BF)
         slope = half + 0.5 * v * (1.0 - t * t) * (C0 * (1.0 + 3.0 * C1 * v2))
-        grad = gbuf[:, b * BLK : (b + 1) * BLK].astype(F32) * slope
-        btotal = btotal + grad
-        narrow = grad.astype(BF)
-        scaled = (grad * inv).astype(BF)
-        right = jnp.concatenate(
-            [
-                jnp.concatenate([narrow, nothing], axis=1),
-                jnp.concatenate([nothing, scaled], axis=1),
-            ],
-            axis=0,
+        grad = gbuf[:, at].astype(F32) * slope
+        narrow[b] = grad.astype(BF)
+        scaled[b] = (grad * inv).astype(BF)
+        return btotal + grad
+
+    btotal = lax.fori_loop(0, RB, activate, jnp.zeros((HU, BLK), F32), unroll=True)
+    lefts, rights = [], []
+    for b in range(RB):
+        lefts += [ffull[:, :, b].reshape(NF * FR, BLK), ablocks[b]]
+        rights.append(
+            jnp.concatenate(
+                [
+                    jnp.concatenate([narrow[b], nothing], axis=1),
+                    jnp.concatenate([nothing, scaled[b]], axis=1),
+                ],
+                axis=0,
+            )
         )
-        gtotal = gtotal + dot_nt(jnp.concatenate([fb, ab], axis=1), right)
-    hidden_copy = pltpu.make_async_copy(hbuf, hidden_ref, local_sem.at[1])
-    hidden_copy.start()
+    gtotal = dot_nt(jnp.concatenate(lefts, axis=1), jnp.concatenate(rights, axis=1))
+    gscratch[...] = gtotal.reshape(ND, PIECE, BLK)
 
     ones8 = jnp.ones((8, BLK), BF)
     brow = jnp.zeros((8, BLK), F32)
     for part in split3(btotal):
         brow = brow + dot_nt(ones8, jnp.concatenate([part, nothing], axis=0))
-    for g in range(NF):
+    def place_rows(g, c):
         away = lax.rem(g - f + NF, NF)
         odd = away // 4
         near = odd * (7 - away) + (1 - odd) * lax.rem(away + 3, 4)
         for q in range(PIECE):
             p = (q * 4 + near) * 2 + odd
-            at = (q // 2) * NF * HALF + g * HALF + (q % 2) * PIECE
-            gsend[p, :PIECE] = gtotal[at : at + PIECE]
+            gsend[p, :PIECE] = gscratch[(q // 2) * 2 * NF + g * 2 + q % 2]
             gsend[p, PIECE:] = brow[:PIECE]
+        return c
+
+    lax.fori_loop(0, NF, place_rows, 0, unroll=True)
     grecv[d] = gsend[d]
-    for p in OTHERS:
-        e = plane_peer(p)
+    def send_parts(j):
+        e = plane_peer(j)
         remote(gsend.at[e], grecv.at[d], 6, (f, e)).start()
+
+    each(ND - 1, send_parts)
     settle(grecv.at[pl.ds(0, ND - 1)], recv_sem.at[6])
 
     added = grecv[0]
     for e in range(1, ND):
         added = added + grecv[e]
     red[...] = added[:PIECE]
-    biasv[...] = added[PIECE : PIECE + 1, :HU]
-    bias_copy = pltpu.make_async_copy(biasv, biasg_ref, local_sem.at[11])
-    bias_copy.start()
-
-    for p in OTHERS:
-        remote(red, fin.at[f, place], 7, (plane, plane_peer(p))).start()
+    biasg_ref[...] = added[PIECE : PIECE + 1, :HU]
+
+    def send_rows(j):
+        remote(red, fin.at[f, place], 7, (plane, plane_peer(j))).start()
+
+    each(ND - 1, send_rows)
 
     @pl.when(shift != 0)
     def _():
-        remote(red, fin.at[f, place], 7, (plane, d)).start()
+        send_rows(ND - 1)
 
     @pl.when(shift == 0)
     def _():
@@ -367,16 +404,16 @@
     def _():
         settle(flat, recv_sem.at[7])
 
-    rows = [jnp.concatenate([fin[g, q] for q in range(PIECE)], axis=0) for g in range(NF)]
-    for j in range(0, NF, 2):
-        a, b = rows[j], rows[j + 1]
-        at = slice(j * HU, (j + 2) * HU)
-        selfv[:, at] = jnp.concatenate([a[:, :HU], b[:, :HU]], axis=1)
-        neighv[:, at] = jnp.concatenate([a[:, HU:], b[:, HU:]], axis=1)
-    self_copy = pltpu.make_async_copy(selfv, selfg_ref, local_sem.at[12])
-    self_copy.start()
-    neigh_copy = pltpu.make_async_copy(neighv, neighg_ref, local_sem.at[13])
-    neigh_copy.start()
+    def assemble(j, c):
+        a, b = [
+            jnp.concatenate([fin[2 * j + i, q] for q in range(PIECE)], axis=0) for i in range(2)
+        ]
+        at = pl.ds(pl.multiple_of(j * BLK, BLK), BLK)
+        selfg_ref[:, at] = jnp.concatenate([a[:, :HU], b[:, :HU]], axis=1)
+        neighg_ref[:, at] = jnp.concatenate([a[:, HU:], b[:, HU:]], axis=1)
+        return c
+
+    lax.fori_loop(0, NF // 2, assemble, 0, unroll=True)
 
     for h in range(2):
         settle(sendbuf.at[h, pl.ds(0, ND - 1)], send_sem.at[h])
@@ -392,9 +429,6 @@
     @pl.when(shift != 0)
     def _():
         settle(flat, send_sem.at[7])
-
-    for copy in (bias_copy, hidden_copy, self_copy, neigh_copy):
-        copy.wait()
 
 
 def hand_over(*refs):
@@ -444,7 +478,7 @@
             pltpu.VMEM((NS, FR, BLK), BF),
             pltpu.VMEM((TILES, BLK, BLK), BF),
             pltpu.VMEM((RB + 1, MROWS, BLK), BF),
-            pltpu.VMEM((RB + 1, FR, BLK), BF),
+            pltpu.VMEM((MROWS, BLK), F32),
             pltpu.VMEM((2, NF, RB, HALF, BLK), BF),
             pltpu.VMEM((NF, FR, BLK), BF),
             pltpu.VMEM((NF, FR, BLK), BF),
@@ -452,15 +486,15 @@
             pltpu.VMEM((2, RB, HALF, BLK), BF),
             pltpu.VMEM((2, NF, RB, HALF, BLK), BF),
             pltpu.VMEM((RB, HU, BLK), F32),
-            pltpu.VMEM((HU, RB * BLK), BF),
+            pltpu.VMEM((RB, HU, BLK), F32),
+            pltpu.VMEM((RB, HU, BLK), BF),
+            pltpu.VMEM((RB, HU, BLK), BF),
+            pltpu.VMEM((ND, PIECE, BLK), F32),
             pltpu.VMEM((HU, RB * BLK), BF),
             pltpu.VMEM((ND, 8, BLK), F32),
             pltpu.VMEM((ND, 8, BLK), F32),
             pltpu.VMEM((PIECE, BLK), F32),
             pltpu.VMEM((NF, PIECE, PIECE, BLK), F32),
-            pltpu.VMEM((FR, NF * HU), F32),
-            pltpu.VMEM((FR, NF * HU), F32),
-            pltpu.VMEM((1, HU), F32),
             pltpu.SemaphoreType.DMA((TILES // STEP,)),
             pltpu.SemaphoreType.DMA((14,)),
             pltpu.SemaphoreType.DMA((8,)),

time: 45 us -> 43.3 us (0.962)
  Pallas kernels: 43.5 us -> 41.9 us
    pallas_call x1, Pallas kernels: 42.8 us -> 41.2 us  [body(): pl.pallas_call(kernel, out_shape=tuple((pltpu.VMEM(one.shape, one.dtype)...]
where the time goes in v5:
time: 43.3 us; the launch traced here: 43.2 us
  Pallas kernels  41.9 us (97%)
  between operations  1.29 us (3%)
    pallas_call x1, Pallas kernels, body(): pl.pallas_call(kernel, out_shape=tuple((pltpu.VMEM(one.shape, one.dtype)...  41.2 us

profile of v5, /device:TPU:1, one launch (start us, length us, event | category | flops | bytes accessed | tf_op | source)
XLA Modules:
  0.0 43.2 jit_solution(6985747746422270237)
XLA Ops:
  1.3 41.2 %shard_map.138 = (bf16[64,1024]{1,0:T(8,128)(2,1)S(1)}, f32[16,512]{1,0:T(8,128)S(1)}, f32[16,512]{1,0:T(8,128)S(1)}, f32[1,64]{1,0:T(1,128)S(1)}) custom-call(bf16[16,1024]{1,0:T(8,128)(2,1)} %feat_hbm.1, bf16[16,512]{1,0:T(8,128)(2,1)} %sw_hbm.1, bf16[16,512]{1,0:T(8,128)(2,1)} %nw_hbm.1, f32[64]{0:T(128)} %bias_hbm.1, s32[1,4,32]{2,1,0:T(4,128)} %bitcast.4, ...), custom_call_target="tpu_custom_call" | custom-call | tf_op jit(solution)/shard_map/pallas_call | solution.py:460
  42.5 0.7 %shard_map.139 = (bf16[64,1024]{1,0:T(8,128)(2,1)}, f32[16,512]{1,0:T(8,128)}, f32[16,512]{1,0:T(8,128)}, f32[1,64]{1,0:T(1,128)}) custom-call(bf16[64,1024]{1,0:T(8,128)(2,1)S(1)} %get-tuple-element.12.refs_0_, f32[16,512]{1,0:T(8,128)S(1)} %get-tuple-element.13.refs_1_, f32[16,512]{1,0:T(8,128)S(1)} %get-tuple-element.14.refs_2_, ...), custom_call_target="tpu_custom_call" | custom-call | tf_op jit(solution)/shard_map/pallas_call | solution.py:519

commit v6 on v5

--- a/solution.py
+++ b/solution.py
@@ -15,12 +15,12 @@
 NS = 136
 TILES = 256
 STEP = 32
-LONG = 256
+LONG = 128
 FR = 16
 HU = 64
 PIECE = 4
 HALF = FR // 2
-MROWS = RB * HALF
+MROWS = RB * FR
 
 
 def around(n, i):
@@ -89,7 +89,7 @@
     own,
     sendbuf,
     slots,
-    twice,
+    padded,
     wbuf,
     mask,
     inverse,
@@ -231,7 +231,7 @@
 
     row = lax.broadcasted_iota(jnp.int32, (MROWS, BLK), 0)
     for j in range(RB):
-        mask[j] = jnp.where((row >= HALF * j) & (row < HALF * (j + 1)), 1.0, 0.0).astype(BF)
+        mask[j] = jnp.where((row >= FR * j) & (row < FR * (j + 1)), 1.0, 0.0).astype(BF)
     mask[RB] = jnp.zeros((MROWS, BLK), BF)
     live = live_ref[0, 0]
 
@@ -239,7 +239,7 @@
         return jnp.where(t < live, target_ref[0, t], RB)
 
     def fill_ones(i, c):
-        twice[i] = jnp.ones((FR, BLK), BF)
+        padded[i] = jnp.ones((FR, BLK), BF)
         return c
 
     lax.fori_loop(0, NS, fill_ones, 0)
@@ -248,11 +248,9 @@
     wide = jnp.concatenate([wide, jnp.zeros((BLK, BLK - HU), F32)], axis=1)
     bias_cols = jnp.transpose(wide)[:HU]
 
-    def double(h, i, c):
+    def pad(h, i, c):
         for u in range(8):
-            block = slots[h, i * 8 + u]
-            twice[i * 8 + u, :HALF] = block
-            twice[i * 8 + u, HALF:] = block
+            padded[i * 8 + u, :HALF] = slots[h, i * 8 + u]
         return c
 
     def aggregate(turn, c):
@@ -266,14 +264,14 @@
         @pl.when(turn > 0)
         def _():
             settle(slots.at[h, pl.ds(RB, BMAX * (ND - 1))], recv_sem.at[h])
-            lax.fori_loop(0, NS // 8, functools.partial(double, h), 0)
+            lax.fori_loop(0, NS // 8, functools.partial(pad, h), 0)
 
         def step(i, total):
             left, right = [], []
             for u in range(LONG):
                 t = i * LONG + u
-                chosen = twice[source_ref[0, t]]
-                left.append(jnp.concatenate([chosen] * (RB // 2), axis=0) * mask[goal(t)])
+                chosen = padded[source_ref[0, t]]
+                left.append(jnp.concatenate([chosen] * RB, axis=0) * mask[goal(t)])
                 right.append(wbuf[t])
             return total + dot_nt(jnp.concatenate(left, axis=1), jnp.concatenate(right, axis=1))
 
@@ -286,7 +284,7 @@
         @pl.when(turn > 0)
         def _():
             for b in range(RB):
-                block = total[b * HALF : (b + 1) * HALF].astype(BF)
+                block = total[b * FR : b * FR + HALF].astype(BF)
                 abuf[h, b] = block
                 afull[h, f, b] = block
 
@@ -324,7 +322,7 @@
 
     def activate(b, btotal):
         at = pl.ds(pl.multiple_of(b * BLK, BLK), BLK)
-        inv = inverse[pl.ds(pl.multiple_of(b * HALF, HALF), HALF)][:1]
+        inv = inverse[pl.ds(pl.multiple_of(b * FR, FR), HALF)][:1]
         v = ubuf[b] + vbuf[b] * inv
         v2 = v * v
         t = jnp.tanh(C0 * v * (1.0 + C1 * v2))

time: 43.3 us -> 42.5 us (0.982)
  Pallas kernels: 41.9 us -> 41.1 us
    pallas_call x1, Pallas kernels: 41.2 us -> 40.4 us  [body(): pl.pallas_call(kernel, out_shape=tuple((pltpu.VMEM(one.shape, one.dtype)...]
where the time goes in v6:
time: 42.5 us; the launch traced here: 42.4 us
  Pallas kernels  41.1 us (97%)
  between operations  1.29 us (3%)
    pallas_call x1, Pallas kernels, body(): pl.pallas_call(kernel, out_shape=tuple((pltpu.VMEM(one.shape, one.dtype)...  40.4 us

profile of v6, /device:TPU:1, one launch (start us, length us, event | category | flops | bytes accessed | tf_op | source)
XLA Modules:
  0.0 42.4 jit_solution(8532478011142915214)
XLA Ops:
  1.3 40.4 %shard_map.138 = (bf16[64,1024]{1,0:T(8,128)(2,1)S(1)}, f32[16,512]{1,0:T(8,128)S(1)}, f32[16,512]{1,0:T(8,128)S(1)}, f32[1,64]{1,0:T(1,128)S(1)}) custom-call(bf16[16,1024]{1,0:T(8,128)(2,1)} %feat_hbm.1, bf16[16,512]{1,0:T(8,128)(2,1)} %sw_hbm.1, bf16[16,512]{1,0:T(8,128)(2,1)} %nw_hbm.1, f32[64]{0:T(128)} %bias_hbm.1, s32[1,4,32]{2,1,0:T(4,128)} %bitcast.4, ...), custom_call_target="tpu_custom_call" | custom-call | tf_op jit(solution)/shard_map/pallas_call | solution.py:458
  41.7 0.7 %shard_map.139 = (bf16[64,1024]{1,0:T(8,128)(2,1)}, f32[16,512]{1,0:T(8,128)}, f32[16,512]{1,0:T(8,128)}, f32[1,64]{1,0:T(1,128)}) custom-call(bf16[64,1024]{1,0:T(8,128)(2,1)S(1)} %get-tuple-element.12.refs_0_, f32[16,512]{1,0:T(8,128)S(1)} %get-tuple-element.13.refs_1_, f32[16,512]{1,0:T(8,128)S(1)} %get-tuple-element.14.refs_2_, ...), custom_call_target="tpu_custom_call" | custom-call | tf_op jit(solution)/shard_map/pallas_call | solution.py:517

commit v7 on v6

--- a/solution.py
+++ b/solution.py
@@ -227,7 +227,6 @@
         remote(wsend.at[g], wfull.at[f], 2, (g, d)).start()
         remote(own.at[:, pl.ds(0, RB)], ffull.at[:, f], 3, (g, d)).start()
 
-    each(NF - 1, send_inputs)
 
     row = lax.broadcasted_iota(jnp.int32, (MROWS, BLK), 0)
     for j in range(RB):
@@ -280,6 +279,7 @@
         @pl.when(turn == 0)
         def _():
             inverse[...] = 1.0 / (1.0 + total)
+            each(NF - 1, send_inputs)
 
         @pl.when(turn > 0)
         def _():
@@ -350,10 +350,9 @@
     gtotal = dot_nt(jnp.concatenate(lefts, axis=1), jnp.concatenate(rights, axis=1))
     gscratch[...] = gtotal.reshape(ND, PIECE, BLK)
 
-    ones8 = jnp.ones((8, BLK), BF)
-    brow = jnp.zeros((8, BLK), F32)
-    for part in split3(btotal):
-        brow = brow + dot_nt(ones8, jnp.concatenate([part, nothing], axis=0))
+    terms = [jnp.concatenate([part, nothing], axis=0) for part in split3(btotal)]
+    brow = dot_nt(jnp.ones((8, 3 * BLK), BF), jnp.concatenate(terms, axis=1))
+
     def place_rows(g, c):
         away = lax.rem(g - f + NF, NF)
         odd = away // 4

time: 42.5 us -> 43.3 us (1.019)
  Pallas kernels: 41.1 us -> 41.9 us
    pallas_call x1, Pallas kernels: 40.4 us -> 41.2 us  [body(): pl.pallas_call(kernel, out_shape=tuple((pltpu.VMEM(one.shape, one.dtype)...]
where the time goes in v7:
time: 43.3 us; the launch traced here: 43.2 us
  Pallas kernels  41.9 us (97%)
  between operations  1.29 us (3%)
    pallas_call x1, Pallas kernels, body(): pl.pallas_call(kernel, out_shape=tuple((pltpu.VMEM(one.shape, one.dtype)...  41.2 us

profile of v7, /device:TPU:1, one launch (start us, length us, event | category | flops | bytes accessed | tf_op | source)
XLA Modules:
  0.0 43.2 jit_solution(3267697599457195579)
XLA Ops:
  1.3 41.2 %shard_map.138 = (bf16[64,1024]{1,0:T(8,128)(2,1)S(1)}, f32[16,512]{1,0:T(8,128)S(1)}, f32[16,512]{1,0:T(8,128)S(1)}, f32[1,64]{1,0:T(1,128)S(1)}) custom-call(bf16[16,1024]{1,0:T(8,128)(2,1)} %feat_hbm.1, bf16[16,512]{1,0:T(8,128)(2,1)} %sw_hbm.1, bf16[16,512]{1,0:T(8,128)(2,1)} %nw_hbm.1, f32[64]{0:T(128)} %bias_hbm.1, s32[1,4,32]{2,1,0:T(4,128)} %bitcast.4, ...), custom_call_target="tpu_custom_call" | custom-call | tf_op jit(solution)/shard_map/pallas_call | solution.py:457
  42.5 0.7 %shard_map.139 = (bf16[64,1024]{1,0:T(8,128)(2,1)}, f32[16,512]{1,0:T(8,128)}, f32[16,512]{1,0:T(8,128)}, f32[1,64]{1,0:T(1,128)}) custom-call(bf16[64,1024]{1,0:T(8,128)(2,1)S(1)} %get-tuple-element.12.refs_0_, f32[16,512]{1,0:T(8,128)S(1)} %get-tuple-element.13.refs_1_, f32[16,512]{1,0:T(8,128)S(1)} %get-tuple-element.14.refs_2_, ...), custom_call_target="tpu_custom_call" | custom-call | tf_op jit(solution)/shard_map/pallas_call | solution.py:516
